TPU v7x, 32 devices: a whole 2x2x4 slice. The times are simulated.
32 devices in a mesh: dp: 4 (over y, x), seq: 8 (over z, core).
Axes of the slice: x: 2, y: 2, z: 4, core: 2. Of those that a mesh axis runs over, the one named last changes fastest.
Arguments:
- features: bfloat16 [32, 16, 32, 512], P('dp', 'seq'), may hold values from -6 to 6
- conv_weight: bfloat16 [3, 3, 3, 16, 512], replicated, may hold values from -0.0546875 to 0.0546875
- clip_frames: int32 [8], replicated, may hold values from 1 to 7, as said below
- clip_group: int32 [8], replicated, may hold values from 0 to 3, as said below
- clip_offset: int32 [8], replicated, may hold values from 0 to 7, as said below
- clip_times: float32 [8], replicated, may hold values from 0.05 to 0.95
- noise_tokens: bfloat16 [4, 1024, 64], P('dp', 'seq'), may hold values from -6 to 6
- embed_weight: bfloat16 [64, 2048], replicated, may hold values from -0.75 to 0.75
- attention_proj: bfloat16 [2048, 3, 8, 128], P(None, None, 'seq'), may hold values from -0.125 to 0.125
- norm_gains: float32 [2, 128], replicated, may hold values from 0.5 to 1.5
- cotangent: bfloat16 [4, 1024, 1024], P('dp', 'seq'), may hold values from -0.09375 to 0.09375
Outputs:
- noisy_tokens: float32 [4, 1024, 64], P('dp', 'seq')
- attention_out: bfloat16 [4, 1024, 1024], P('dp', 'seq')
- proj_grad: float32 [2048, 3, 8, 128], P('dp', None, 'seq')
- norm_grad: float32 [2, 128], replicated
Inputs may be any that keep to these rules, and one draw needn't show every extreme that they name: `clip_frames`: clips follow one another along time from frame 0 and together cover all 32 frames. `clip_group`: every group trains on exactly two clips, whose frames add up to 8. `clip_offset`: the clips of one group take consecutive frame slots from slot 0 in their time order and fill all 8 slots of the group.
All inputs are finite; a program needn't handle non-finite values.
Results may differ from a plain program's by a relative error of at most 0.014.
Values may be sent and summed in bfloat16 or wider, within the bound.
No kernel may reach another device: no remote copies, remote signals or barrier semaphores. Data moves between devices by JAX's collectives and lax.ppermute only.
A program may use at most 128 MiB of HBM per device.

v0:
```python
import functools

import jax
import jax.numpy as jnp
from jax import lax
from jax.experimental import pallas as pl
from jax.experimental.pallas import tpu as pltpu
from jax.sharding import PartitionSpec as P


F32 = jnp.float32
BF16 = jnp.bfloat16
LOG2E = 1.4426950408889634
EPS = 1e-06
BIG = 16384.0
CELLS = ((0, 0), (0, 1), (1, 0), (1, 1), (2, 0), (2, 1), (-1, 0), (-1, 1))
NT = (((1,), (1,)), ((), ()))
TN = (((0,), (0,)), ((), ()))


def swap(block, axis, mask):
    return lax.ppermute(block, axis, [(i, i ^ mask) for i in range(lax.axis_size(axis))])


def keep_in(space, *arrays):
    return [pltpu.with_memory_space_constraint(a, space) for a in arrays]


def cost(flops, moved, exps=0):
    return pl.CostEstimate(flops=int(flops), bytes_accessed=int(moved), transcendentals=int(exps))


def params(mib=48):
    return pltpu.CompilerParams(vmem_limit_bytes=mib * 1024 * 1024)


VMEM = pl.BlockSpec(memory_space=pltpu.VMEM)
HBM = pl.BlockSpec(memory_space=pltpu.HBM)


def split(x):
    high = x.astype(BF16)
    return high, (x - high.astype(F32)).astype(BF16)


def split_kernel(dims, cot_hbm, cots_ref, sems):
    n_seq, head = dims
    loads = [
        pltpu.make_async_copy(
            cot_hbm.at[:, h * head : (h + 1) * head], cots_ref.at[h], sems.at[h]
        )
        for h in range(n_seq)
    ]
    for load in loads:
        load.start()
    for load in loads:
        load.wait()


def conv_kernel(dims, frames_hbm, feat_hbm, w_hbm, part_ref, *rest):
    fr, wd, ch, lat, clips = dims
    frames_ref, feat_ref, w_ref, act_ref, wst_ref, sems = rest
    cols = wd // 2
    slab = lax.axis_index("dp")
    loads = [
        pltpu.make_async_copy(w_hbm, w_ref, sems.at[0]),
        pltpu.make_async_copy(feat_hbm, feat_ref, sems.at[1]),
        pltpu.make_async_copy(frames_hbm, frames_ref, sems.at[2]),
    ]
    for load in loads:
        load.start()
    loads[0].wait()
    lanes = len(CELLS) * lat
    for row in range(2):
        for par in range(2):
            for dt in range(3):
                for blk in range(2):
                    for g, (out_row, out_par) in enumerate(CELLS):
                        dr = row - out_row
                        valid = abs(dr) <= 1
                        dw = par - out_par
                        if blk == 1:
                            valid = valid and dw != 0
                            dw = -dw
                        at = (dt * 2 + blk) * lanes + g * lat
                        tap = ((2 - dt) * 3 + dr + 1) * 3 + dw + 1
                        wst_ref[row * 2 + par, at : at + lat, :] = (
                            w_ref[tap * lat : (tap + 1) * lat, :]
                            if valid
                            else jnp.zeros((lat, ch), BF16)
                        )
    loads[1].wait()
    raw = feat_ref[...].astype(F32)
    act = raw / (1.0 + jnp.exp(-raw))
    for i in range(ch // 128):
        act_ref[i] = act[:, i * 128 : (i + 1) * 128]
    half = fr * 2 * cols
    total = None
    for par in range(2):
        mine = jnp.concatenate(
            [
                act_ref[i, pl.ds(par, half, stride=2), :].astype(BF16)
                for i in range(ch // 128)
            ],
            axis=1,
        ).reshape(fr, 2, cols, ch)
        for row in range(2):
            term = lax.dot_general(
                mine[:, row].reshape(fr * cols, ch),
                wst_ref[row * 2 + par],
                NT,
                preferred_element_type=F32,
            )
            total = term if total is None else total + term
    loads[2].wait()
    starts = [jnp.int32(0)] * (fr + 2)
    begin = jnp.int32(0)
    for c in range(clips):
        end = begin + frames_ref[c]
        for f in range(fr + 2):
            t = slab * fr + f
            starts[f] = jnp.where((t >= begin) & (t < end), begin, starts[f])
        begin = end
    sums = []
    for blk in range(2):
        pieces = []
        for f in range(fr + 2):
            piece = jnp.zeros((cols, lanes), F32)
            for dt in range(3):
                src = f - dt
                if 0 <= src < fr:
                    keep = (slab * fr + src >= starts[f]).astype(F32)
                    at = (dt * 2 + blk) * lanes
                    piece = piece + keep * total[src * cols : (src + 1) * cols, at : at + lanes]
            pieces.append(piece)
        sums.append(jnp.concatenate(pieces, axis=0))
    same, side = sums
    rows = (fr + 2) * cols
    col_at = lax.broadcasted_iota(jnp.int32, (rows, lanes), 0) % cols
    par_at = (lax.broadcasted_iota(jnp.int32, (rows, lanes), 1) // lat) % 2
    after = jnp.where(col_at < cols - 1, pltpu.roll(side, rows - 1, 0), 0.0)
    before = jnp.where(col_at > 0, pltpu.roll(side, 1, 0), 0.0)
    part_ref[...] = (same + jnp.where(par_at == 1, after, before)).astype(BF16)


def table_kernel(dims, after_ref, frames_hbm, group_hbm, offset_hbm, times_hbm, noise_hbm, *rest):
    fr, cols, clips, n_dp, patch, width = dims
    pick_ref, scale_ref, noise_ref, live_ref, mark_ref = rest[:5]
    frames_ref, group_ref, offset_ref, times_ref, raw_ref, sems = rest[5:]
    loads = [
        pltpu.make_async_copy(source, target, sems.at[i])
        for i, (source, target) in enumerate(
            (
                (frames_hbm, frames_ref),
                (group_hbm, group_ref),
                (offset_hbm, offset_ref),
                (times_hbm, times_ref),
                (noise_hbm, raw_ref),
            )
        )
    ]
    for load in loads:
        load.start()
    for load in loads:
        load.wait()
    slab = lax.axis_index("dp")
    source = [jnp.int32(-1)] * fr
    owner = [jnp.int32(clips)] * fr
    level = [jnp.float32(0.0)] * fr
    usable = [jnp.float32(0.0)] * fr
    begin = jnp.int32(0)
    for c in range(clips):
        size, off = frames_ref[c], offset_ref[c]
        here = group_ref[c] == slab
        for f in range(fr):
            member = here & (off <= f) & (f < off + size)
            source[f] = jnp.where(member, begin + f - off, source[f])
            owner[f] = jnp.where(member, c, owner[f])
            usable[f] = jnp.where(member, 1.0, usable[f])
            level[f] = jnp.where(member, times_ref[c], level[f])
        begin = begin + size
    rows = (fr + 2) * cols
    noise = raw_ref[...].astype(F32).T
    noise = jnp.concatenate([noise, jnp.zeros((fr * cols, width - patch), F32)], axis=1)
    ahead = lax.broadcasted_iota(jnp.int32, (cols, n_dp * rows), 1) - lax.broadcasted_iota(
        jnp.int32, (cols, n_dp * rows), 0
    )
    lane = lax.broadcasted_iota(jnp.int32, (cols, width), 1)
    for f in range(fr):
        here = slice(f * cols, (f + 1) * cols)
        hit = None
        for m in range(n_dp):
            at = source[f] - (slab ^ m) * fr
            valid = (at >= 0) & (at < fr + 2) & (source[f] >= 0)
            at = jnp.where(valid, m * rows + at * cols, -cols)
            hit = (ahead == at) if hit is None else hit | (ahead == at)
        pick_ref[here, :] = hit.astype(F32).astype(BF16)
        scale_ref[here, :] = jnp.full((cols, width), usable[f] * (1.0 - level[f]), F32)
        noise_ref[here, :] = (usable[f] * level[f]) * noise[here]
        live_ref[here, :] = jnp.full((cols, width), usable[f], F32)
        mark_ref[here, :] = (lane == owner[f]).astype(F32)


def slot_kernel(dims, pick_ref, scale_ref, noise_ref, *rest):
    (n_dp,) = dims
    part_refs, (send_ref, own_ref) = rest[:n_dp], rest[n_dp:]
    parts = jnp.concatenate([ref[...] for ref in part_refs], axis=0)
    got = jnp.dot(pick_ref[...], parts, preferred_element_type=F32)
    own = scale_ref[...] * got + noise_ref[...]
    own_ref[...] = own
    send_ref[...] = own.astype(BF16)


def weight_kernel(dims, after_ref, embed_hbm, proj_hbm, gains_hbm, out_ref, gains_ref, *rest):
    patch, head = dims
    embed_ref, proj_ref, sems = rest
    loads = [
        pltpu.make_async_copy(embed_hbm, embed_ref, sems.at[0]),
        pltpu.make_async_copy(gains_hbm, gains_ref, sems.at[1]),
    ] + [pltpu.make_async_copy(proj_hbm.at[i], proj_ref.at[i], sems.at[2 + i]) for i in range(3)]
    for load in loads:
        load.start()
    loads[0].wait()
    for i in range(3):
        loads[2 + i].wait()
        both = jnp.dot(embed_ref[...], proj_ref[i], preferred_element_type=F32)
        high, low = split(both)
        out_ref[:patch, i * head : (i + 1) * head] = high
        out_ref[patch:, i * head : (i + 1) * head] = low
    loads[1].wait()


def mean_of(values, head):
    ones = jnp.full((2 * head, head), 1.0 / head, BF16)
    return jnp.dot(jnp.concatenate(split(values), axis=1), ones, preferred_element_type=F32)


def attention_kernel(dims, gains_ref, w_ref, own_ref, live_ref, mark_ref, cots_ref, *rest):
    fr, cols, n_seq, patch, head, tile, devices = dims
    tok_refs, rest = rest[:n_seq], rest[n_seq:]
    noisy_ref, grad_ref, gain_ref = rest[:3]
    pairs_refs, rest = rest[3 : 3 + n_seq // 2], rest[3 + n_seq // 2 :]
    tok_ref, toks_ref, x_ref, q_ref, k_ref, v_ref, o_ref, dq_ref, dk_ref, dv_ref = rest
    me = lax.axis_index("seq")
    blk = fr * cols
    size = n_seq * blk
    width = 2 * patch
    tok_ref[:blk, :] = jnp.zeros((blk, width), BF16)
    tok_ref[size + blk :, :] = jnp.zeros((blk, width), BF16)
    for m in range(n_seq):
        at = pl.multiple_of((me ^ m) * blk, blk)
        tok_ref[pl.ds(at + blk, blk), :] = tok_refs[m][...]
    own_at = pl.multiple_of(me * blk, blk)
    lane = lax.broadcasted_iota(jnp.int32, (blk, width), 1)
    side = jnp.where(
        lane < patch + patch // 2,
        tok_ref[pl.ds(own_at, blk), :].astype(F32),
        tok_ref[pl.ds(own_at + 2 * blk, blk), :].astype(F32),
    )
    noisy = own_ref[...] + pltpu.roll(side, patch, 1)
    noisy_ref[...] = noisy.T[:patch, :]
    weights = w_ref[...]
    mark = mark_ref[...]
    for p in range(n_seq):
        rows = slice(p * blk, (p + 1) * blk)
        side = jnp.where(
            lane < patch + patch // 2,
            tok_ref[rows, :].astype(F32),
            tok_ref[(p + 2) * blk : (p + 3) * blk, :].astype(F32),
        )
        tok = tok_ref[(p + 1) * blk : (p + 2) * blk, :].astype(F32) + pltpu.roll(side, patch, 1)
        tok = jnp.where(lane < patch, tok, pltpu.roll(tok, patch, 1)).astype(BF16)
        toks_ref[rows, :] = tok
        x = jnp.dot(tok, weights, preferred_element_type=F32)
        x_ref[rows, :] = x
        scale = lax.rsqrt(mean_of(x[:, :head] * x[:, :head], head) + EPS)
        gain = gains_ref[0:1, :] * (head**-0.5 * LOG2E)
        q_ref[rows, :head] = (x[:, :head] * scale * gain).astype(BF16)
        q_ref[rows, head:] = mark.astype(BF16)
        x = x[:, head:]
        scale = lax.rsqrt(mean_of(x[:, :head] * x[:, :head], head) + EPS)
        k_ref[rows, :head] = (x[:, :head] * scale * gains_ref[1:2, :]).astype(BF16)
        k_ref[rows, head:] = ((mark - 1.0) * BIG).astype(BF16)
        v_ref[rows, :head] = x[:, head:].astype(BF16)
        v_ref[rows, head:] = jnp.ones((blk, head), BF16)
    per = tile // blk
    live = jnp.concatenate([live_ref[...]] * per, axis=0)
    for i in range(size // tile):
        rows = slice(i * tile, (i + 1) * tile)
        scores = lax.dot_general(q_ref[rows, :], k_ref[...], NT, preferred_element_type=F32)
        exps = jnp.exp2(scores)
        exps_bf = exps.astype(BF16)
        both = jnp.dot(exps_bf, v_ref[...], preferred_element_type=F32)
        inverse = 1.0 / both[:, head:]
        output = both[:, :head] * inverse
        o_ref[rows, :] = (output * live).astype(BF16)
        incoming = cots_ref[i * per : (i + 1) * per].reshape(tile, head)
        scaled = incoming.astype(F32) * live * inverse
        scaled_bf = scaled.astype(BF16)
        upstream = jnp.concatenate([scaled_bf, (-(scaled * output)).astype(BF16)], axis=1)
        prob_grad = lax.dot_general(upstream, v_ref[...], NT, preferred_element_type=F32)
        score_grad = (exps * prob_grad).astype(BF16)
        dq_ref[rows, :] = jnp.dot(score_grad, k_ref[:, :head], preferred_element_type=F32)
        dk = lax.dot_general(score_grad, q_ref[rows, :head], TN, preferred_element_type=F32)
        dv = lax.dot_general(exps_bf, scaled_bf, TN, preferred_element_type=F32)
        if i == 0:
            dk_ref[...] = dk
            dv_ref[...] = dv
        else:
            dk_ref[...] += dk
            dv_ref[...] += dv

    gains = []
    grad = None
    for p in range(n_seq):
        rows = slice(p * blk, (p + 1) * blk)
        parts = []
        for i, (ref, unit) in enumerate(((dq_ref, head**-0.5), (dk_ref, 1.0 / LOG2E))):
            x = x_ref[rows, i * head : (i + 1) * head]
            up = ref[rows, :] * unit
            scale = lax.rsqrt(mean_of(x * x, head) + EPS)
            unit_x = x * scale
            gain_up = up * gains_ref[i : i + 1, :]
            parts.append((scale * (gain_up - unit_x * mean_of(unit_x * gain_up, head))).astype(BF16))
            add = jnp.sum(up * unit_x, axis=0, keepdims=True)
            if p == 0:
                gains.append(add)
            else:
                gains[i] = gains[i] + add
        parts.append(dv_ref[rows, :].astype(BF16))
        term = lax.dot_general(
            toks_ref[rows, :], jnp.concatenate(parts, axis=1), TN, preferred_element_type=F32
        )
        grad = term if grad is None else grad + term
    grad_ref[...] = grad[:patch, :].astype(BF16)
    gain_ref[...] = jnp.broadcast_to(jnp.concatenate(gains, axis=0)[None], (devices, 2, head))
    for m in range(n_seq):
        at = pl.multiple_of((me ^ m) * blk, blk)
        pairs_refs[m // 2][m % 2] = o_ref[pl.ds(at, blk), :]


def proj_kernel(dims, embed_ref, *rest):
    n_dp, _, head, rows = dims
    grad_refs, (out_ref,) = rest[:n_dp], rest[n_dp:]
    slab = lax.axis_index("dp")
    part = embed_ref[:, pl.ds(pl.multiple_of(slab * rows, rows), rows)]
    left = jnp.concatenate([part] * n_dp, axis=0)
    right = jnp.concatenate([ref[...] for ref in grad_refs], axis=0)
    result = lax.dot_general(left, right, TN, preferred_element_type=F32)
    for i in range(3):
        out_ref[pl.ds(i, rows, stride=3), :] = result[:, i * head : (i + 1) * head]


def finish_kernel(dims, sums_ref, *rest):
    n_seq, head = dims
    own_refs, other_refs, (out_ref, gain_ref) = rest[: n_seq // 2], rest[n_seq // 2 : n_seq], rest[n_seq:]
    me = lax.axis_index("seq")
    for m in range(n_seq):
        at = pl.multiple_of((me ^ m) * head, head)
        source = other_refs if m % 2 else own_refs
        out_ref[:, pl.ds(at, head)] = source[m // 2][m % 2]
    gain_ref[...] = jnp.sum(sums_ref[...], axis=0)


def body(
    features,
    conv_weight,
    clip_frames,
    clip_group,
    clip_offset,
    clip_times,
    noise_tokens,
    embed_weight,
    attention_proj,
    norm_gains,
    cotangent,
):
    n_dp, n_seq = lax.axis_size("dp"), lax.axis_size("seq")
    fr, rows_dev, wd, ch = features.shape
    lat = conv_weight.shape[3]
    clips = clip_frames.shape[0]
    cols = wd // 2
    blk, patch = noise_tokens.shape[1:]
    model, _, heads_dev, head = attention_proj.shape
    assert rows_dev == 2 and heads_dev == 1 and blk == fr * cols and patch == 4 * lat
    size = n_seq * blk
    lanes = len(CELLS) * lat
    S = jax.ShapeDtypeStruct

    rows_out = (fr + 2) * cols
    tile = min(256, size)
    devices = n_dp * n_seq
    gather = dict(split_axis=0, concat_axis=0, tiled=True)

    cots = pl.pallas_call(
        functools.partial(split_kernel, (n_seq, head)),
        out_shape=S((n_seq, blk, head), BF16),
        in_specs=[HBM],
        out_specs=VMEM,
        scratch_shapes=[pltpu.SemaphoreType.DMA((n_seq,))],
        compiler_params=params(),
        cost_estimate=cost(0, 4 * blk * n_seq * head),
        name="split",
    )(*keep_in(pltpu.HBM, cotangent.reshape(blk, n_seq * head)))
    cots = lax.all_to_all(cots, "seq", **gather)

    partial = pl.pallas_call(
        functools.partial(conv_kernel, (fr, wd, ch, lat, clips)),
        out_shape=S((rows_out, lanes), BF16),
        in_specs=[HBM] * 3,
        out_specs=VMEM,
        scratch_shapes=[
            pltpu.SMEM((clips,), jnp.int32),
            pltpu.VMEM((fr * 2 * wd, ch), BF16),
            pltpu.VMEM((27 * lat, ch), BF16),
            pltpu.VMEM((ch // 128, fr * 2 * wd, 128), F32),
            pltpu.VMEM((4, 6 * lanes, ch), BF16),
            pltpu.SemaphoreType.DMA((3,)),
        ],
        compiler_params=params(),
        cost_estimate=cost(2 * fr * cols * 4 * ch * 6 * lanes, 2**21, fr * 2 * wd * ch),
        name="conv",
    )(
        *keep_in(
            pltpu.HBM,
            clip_frames,
            features.reshape(fr * 2 * wd, ch),
            conv_weight.reshape(27 * lat, ch),
        )
    )
    parts = [partial] + [swap(partial, "dp", m) for m in range(1, n_dp)]
    pick, scale, noise, live, mark = pl.pallas_call(
        functools.partial(table_kernel, (fr, cols, clips, n_dp, patch, lanes)),
        out_shape=[S((blk, n_dp * rows_out), BF16)] + [S((blk, lanes), F32)] * 4,
        in_specs=[VMEM] + [HBM] * 5,
        out_specs=[VMEM] * 5,
        scratch_shapes=[pltpu.SMEM((clips,), jnp.int32)] * 3
        + [
            pltpu.SMEM((clips,), F32),
            pltpu.VMEM((patch, blk), BF16),
            pltpu.SemaphoreType.DMA((5,)),
        ],
        compiler_params=params(),
        cost_estimate=cost(2**22, 2**21),
        name="tables",
    )(partial, clip_frames, clip_group, clip_offset, clip_times, noise_tokens[0].T)

    send, own = pl.pallas_call(
        functools.partial(slot_kernel, (n_dp,)),
        out_shape=[S((blk, lanes), BF16), S((blk, lanes), F32)],
        in_specs=[VMEM] * (3 + n_dp),
        out_specs=[VMEM] * 2,
        compiler_params=params(),
        cost_estimate=cost(2**20, 2**18),
        name="slots",
    )(pick, scale, noise, *parts)
    toks = [send] + [None] * (n_seq - 1)
    for m in range(2, n_seq, 2):
        toks[m] = swap(send, "seq", m)
    for m in range(0, n_seq, 2):
        toks[m + 1] = swap(toks[m], "seq", 1)
    weights, gains = pl.pallas_call(
        functools.partial(weight_kernel, (patch, head)),
        out_shape=[S((2 * patch, 3 * head), BF16), S((2, head), F32)],
        in_specs=[VMEM] + [HBM] * 3,
        out_specs=[VMEM] * 2,
        scratch_shapes=[
            pltpu.VMEM((patch, model), BF16),
            pltpu.VMEM((3, model, head), BF16),
            pltpu.SemaphoreType.DMA((5,)),
        ],
        compiler_params=params(),
        cost_estimate=cost(2 * patch * model * 3 * head, 2 * model * (3 * head + patch)),
        name="weights",
    )(send, embed_weight, attention_proj.transpose(1, 2, 0, 3).reshape(3, model, head), norm_gains)

    wide = 2 * head
    noisy, grad, gain, *pairs = pl.pallas_call(
        functools.partial(attention_kernel, (fr, cols, n_seq, patch, head, tile, devices)),
        out_shape=[S((patch, blk), F32), S((patch, 3 * head), BF16), S((devices, 2, head), F32)]
        + [S((2, blk, head), BF16)] * (n_seq // 2),
        in_specs=[VMEM] * (6 + n_seq),
        out_specs=[VMEM] * (3 + n_seq // 2),
        scratch_shapes=[
            pltpu.VMEM((size + 2 * blk, lanes), BF16),
            pltpu.VMEM((size, lanes), BF16),
            pltpu.VMEM((size, 3 * head), F32),
            pltpu.VMEM((size, wide), BF16),
            pltpu.VMEM((size, wide), BF16),
            pltpu.VMEM((size, wide), BF16),
            pltpu.VMEM((size, head), BF16),
            pltpu.VMEM((size, head), F32),
            pltpu.VMEM((size, head), F32),
            pltpu.VMEM((size, head), F32),
        ],
        compiler_params=params(),
        cost_estimate=cost(12 * size * size * head, 2**21, size * size),
        name="attention",
    )(gains, weights, own, live, mark, cots, *toks)

    grads = [grad] + [swap(grad, "dp", m) for m in range(1, n_dp)]
    gain_all = lax.all_to_all(gain, ("dp", "seq"), **gather)
    pairs = [pairs[0]] + [swap(pairs[m], "seq", 2 * m) for m in range(1, n_seq // 2)]
    others = [swap(pair, "seq", 1) for pair in pairs]
    rows = model // n_dp
    proj_grad = pl.pallas_call(
        functools.partial(proj_kernel, (n_dp, patch, head, rows)),
        out_shape=S((rows * 3, head), F32),
        in_specs=[VMEM] * (1 + n_dp),
        out_specs=VMEM,
        compiler_params=params(),
        cost_estimate=cost(2 * rows * 3 * head * patch * n_dp, 4 * rows * 3 * head),
        name="projgrad",
    )(embed_weight, *grads)
    out, norm_grad = pl.pallas_call(
        functools.partial(finish_kernel, (n_seq, head)),
        out_shape=[S((blk, n_seq * head), BF16), S((2, head), F32)],
        in_specs=[VMEM] * (1 + n_seq),
        out_specs=[VMEM] * 2,
        compiler_params=params(),
        cost_estimate=cost(0, 4 * blk * n_seq * head),
        name="finish",
    )(gain_all, *pairs, *others)
    return (
        noisy.T[None],
        out[None],
        proj_grad.reshape(rows, 3, heads_dev, head),
        norm_grad,
    )


def solution(mesh):
    return jax.shard_map(
        body,
        mesh=mesh,
        in_specs=(
            P("dp", "seq", None, None),
            P(),
            P(),
            P(),
            P(),
            P(),
            P("dp", "seq", None),
            P(),
            P(None, None, "seq", None),
            P(),
            P("dp", "seq", None),
        ),
        out_specs=(P("dp", "seq", None), P("dp", "seq", None), P("dp", None, "seq", None), P()),
        check_vma=False,
    )
```

profile of v0, /device:TPU:0, one launch (start us, length us, event | category | flops | bytes accessed | tf_op | source)
XLA Modules:
  0.0 58.7 jit_solution(16175626507819795380)
XLA Ops:
  0.6 0.0 copy-start.4
  0.7 1.8 %split.1 = bf16[8,128,128]{2,1,0:T(8,128)(2,1)} custom-call(bf16[128,1024]{1,0:T(8,128)(2,1)} %bitcast.19), custom_call_target="tpu_custom_call" | custom-call | bytes 524288 | tf_op jit(solution)/shard_map/split/pallas_call | solution.py:395
  2.5 6.4 %all-to-all-start = ((bf16[8,128,128]{2,1,0:T(8,128)(2,1)}), bf16[8,128,128]{2,1,0:T(8,128)(2,1)S(1)}, u32[]{:S(2)}, u32[]{:S(2)}) async-start(bf16[8,128,128]{2,1,0:T(8,128)(2,1)} %split.1), calls=%async_computation | async-start | bytes 524288 | tf_op jit(solution)/shard_map/all_to_all | solution.py:405
  8.9 2.6 %conv.1.after_ref.rest_0_ = bf16[160,128]{1,0:T(8,128)(2,1)S(1)} custom-call(s32[8]{0:T(128)} %frames_hbm.3, bf16[512,512]{1,0:T(8,128)(2,1)} %bitcast.20, bf16[432,512]{1,0:T(8,128)(2,1)} %bitcast.21), custom_call_target="tpu_custom_call" | custom-call | flops 402653184 | bytes 2097152 | tf_op jit(solution)/shard_map/conv/pallas_call | solution.py:407
  11.4 2.5 %collective-permute-start.2 = (bf16[160,128]{1,0:T(8,128)(2,1)S(1)}, bf16[160,128]{1,0:T(8,128)(2,1)S(1)}, u32[]{:S(2)}, u32[]{:S(2)}) collective-permute-start(bf16[160,128]{1,0:T(8,128)(2,1)S(1)} %conv.1.after_ref.rest_0_), channel_id=1, source_target_pairs={{0,24},{8,16},{16,8},{24,0},{1,25},{9,17},{17,9},{25,1},{2,26},{10... | collective-permute-start | bytes 122888 | tf_op jit(solution)/shard_map/ppermute | solution.py:22
  13.9 0.5 collective-permute-start.1
  14.4 0.5 collective-permute-start
  15.0 1.1 %tables.1 = (bf16[128,640]{1,0:T(8,128)(2,1)S(1)}, f32[128,128]{1,0:T(8,128)S(1)}, f32[128,128]{1,0:T(8,128)S(1)}, f32[128,128]{1,0:T(8,128)S(1)}, f32[128,128]{1,0:T(8,128)S(1)}) custom-call(bf16[160,128]{1,0:T(8,128)(2,1)S(1)} %conv.1.after_ref.rest_0_, s32[8]{0:T(128)S(1)} %copy-done.4, s32[8]{0:T(128)S(1)} %copy-done.5, s32[8]{0:T(128)S(1)} %copy-done.6, ...), custom_call_target="tpu_custom_call" | custom-call | flops 4194304 | bytes 2097152 | tf_op jit(solution)/shard_map/tables/pallas_call | solution.py:432
  16.1 0.3 collective-permute-done.2.rest_3_
  16.4 1.5 %collective-permute-done.1.rest_2_ = bf16[160,128]{1,0:T(8,128)(2,1)S(1)} collective-permute-done((bf16[160,128]{1,0:T(8,128)(2,1)S(1)}, bf16[160,128]{1,0:T(8,128)(2,1)S(1)}, u32[]{:S(2)}, u32[]{:S(2)}) %collective-permute-start.1) | collective-permute-done | bytes 40992 | tf_op jit(solution)/shard_map/ppermute | solution.py:22
  17.9 0.5 collective-permute-done.rest_1_
  18.5 0.2 slots.1
  18.7 3.9 %collective-permute-start.8 = (bf16[128,128]{1,0:T(8,128)(2,1)S(1)}, bf16[128,128]{1,0:T(8,128)(2,1)S(1)}, u32[]{:S(2)}, u32[]{:S(2)}) collective-permute-start(bf16[128,128]{1,0:T(8,128)(2,1)S(1)} %get-tuple-element.25.after_ref.rest_0_), channel_id=1, source_target_pairs={{0,6},{1,7},{2,4},{3,5},{4,2},{5,3},{6,0},{7,1},{8,14},{9,15},{10,... | collective-permute-start | bytes 98312 | tf_op jit(solution)/shard_map/ppermute | solution.py:22
  22.5 0.0 collective-permute-start.6
  22.5 0.6 %collective-permute-start.4 = (bf16[128,128]{1,0:T(8,128)(2,1)S(1)}, bf16[128,128]{1,0:T(8,128)(2,1)S(1)}, u32[]{:S(2)}, u32[]{:S(2)}) collective-permute-start(bf16[128,128]{1,0:T(8,128)(2,1)S(1)} %get-tuple-element.25.after_ref.rest_0_), channel_id=1, source_target_pairs={{0,2},{1,3},{2,0},{3,1},{4,6},{5,7},{6,4},{7,5},{8,10},{9,11},{10,... | collective-permute-start | bytes 98312 | tf_op jit(solution)/shard_map/ppermute | solution.py:22
  23.2 0.0 collective-permute-start.3
  23.2 1.3 %collective-permute-done.8.rest_6_ = bf16[128,128]{1,0:T(8,128)(2,1)S(1)} collective-permute-done((bf16[128,128]{1,0:T(8,128)(2,1)S(1)}, bf16[128,128]{1,0:T(8,128)(2,1)S(1)}, u32[]{:S(2)}, u32[]{:S(2)}) %collective-permute-start.8) | collective-permute-done | bytes 32800 | tf_op jit(solution)/shard_map/ppermute | solution.py:22
  24.5 2.9 %collective-permute-done.6.rest_4_ = bf16[128,128]{1,0:T(8,128)(2,1)S(1)} collective-permute-done((bf16[128,128]{1,0:T(8,128)(2,1)S(1)}, bf16[128,128]{1,0:T(8,128)(2,1)S(1)}, u32[]{:S(2)}, u32[]{:S(2)}) %collective-permute-start.6) | collective-permute-done | bytes 32800 | tf_op jit(solution)/shard_map/ppermute | solution.py:22
  27.4 0.0 collective-permute-done.4.rest_2_
  27.4 0.5 collective-permute-start.5
  27.9 0.9 %weights.1 = (bf16[128,384]{1,0:T(8,128)(2,1)S(1)}, f32[2,128]{1,0:T(2,128)S(1)}) custom-call(bf16[128,128]{1,0:T(8,128)(2,1)S(1)} %get-tuple-element.25.after_ref.rest_0_, bf16[64,2048]{1,0:T(8,128)(2,1)S(1)} %copy-done.1, bf16[3,2048,128]{2,1,0:T(8,128)(2,1)S(1)} %bitcast.16, f32[2,128]{1,0:T(2,128)S(1)} %copy-done.3), custom_call_target="tpu_custom_call" | custom-call | flops 100663296 | bytes 1835008 | tf_op jit(solution)/shard_map/weights/pallas_call | solution.py:462
  28.7 0.0 collective-permute-done.3.rest_1_
  28.8 0.0 collective-permute-done.9.rest_7_
  28.8 0.0 collective-permute-done.5.rest_3_
  28.8 0.0 all-to-all-done.cots_ref
  28.8 8.8 %attention.1 = (f32[64,128]{1,0:T(8,128)}, bf16[64,384]{1,0:T(8,128)(2,1)S(1)}, f32[32,2,128]{2,1,0:T(2,128)}, bf16[2,128,128]{2,1,0:T(8,128)(2,1)S(1)}, bf16[2,...) custom-call(f32[2,128]{1,0:T(2,128)S(1)} %get-tuple-element.26.gains_ref, ...), custom_call_target="tpu_custom_call" | custom-call | flops 1610612736 | bytes 2097152 | tf_op jit(solution)/shard_map/attention/pallas_call | solution.py:478
  37.6 0.0 collective-permute-start.10
  37.6 1.8 %collective-permute-start.11 = (bf16[2,128,128]{2,1,0:T(8,128)(2,1)S(1)}, bf16[2,128,128]{2,1,0:T(8,128)(2,1)S(1)}, u32[]{:S(2)}, u32[]{:S(2)}) collective-permute-start(bf16[2,128,128]{2,1,0:T(8,128)(2,1)S(1)} %get-tuple-element.35), channel_id=1, source_target_pairs={{0,4},{1,5},{2,6},{3,7},{4,0},{5,1},{6,2},{7,3},{8,12},{9,13},{10,... | collective-permute-start | bytes 196616 | tf_op jit(solution)/shard_map/ppermute | solution.py:22
  39.4 2.6 %collective-permute-start.12 = (bf16[2,128,128]{2,1,0:T(8,128)(2,1)S(1)}, bf16[2,128,128]{2,1,0:T(8,128)(2,1)S(1)}, u32[]{:S(2)}, u32[]{:S(2)}) collective-permute-start(bf16[2,128,128]{2,1,0:T(8,128)(2,1)S(1)} %get-tuple-element.36), channel_id=1, source_target_pairs={{0,6},{1,7},{2,4},{3,5},{4,2},{5,3},{6,0},{7,1},{8,14},{9,15},{10,... | collective-permute-start | bytes 196616 | tf_op jit(solution)/shard_map/ppermute | solution.py:22
  42.0 1.5 %collective-permute-start.19 = (bf16[64,384]{1,0:T(8,128)(2,1)S(1)}, bf16[64,384]{1,0:T(8,128)(2,1)S(1)}, u32[]{:S(2)}, u32[]{:S(2)}) collective-permute-start(bf16[64,384]{1,0:T(8,128)(2,1)S(1)} %get-tuple-element.38.rest_0_), channel_id=1, source_target_pairs={{0,24},{8,16},{16,8},{24,0},{1,25},{9,17},{17,9},{25,1},{2,26},{10... | collective-permute-start | bytes 147464 | tf_op jit(solution)/shard_map/ppermute | solution.py:22
  43.5 0.5 collective-permute-start.18
  44.0 3.0 %collective-permute-done.19.rest_3_ = bf16[64,384]{1,0:T(8,128)(2,1)S(1)} collective-permute-done((bf16[64,384]{1,0:T(8,128)(2,1)S(1)}, bf16[64,384]{1,0:T(8,128)(2,1)S(1)}, u32[]{:S(2)}, u32[]{:S(2)}) %collective-permute-start.19) | collective-permute-done | bytes 49184 | tf_op jit(solution)/shard_map/ppermute | solution.py:22
  47.0 0.0 collective-permute-start.13
  47.0 0.0 collective-permute-done.10.rest_1_
  47.0 0.5 collective-permute-start.14
  47.5 0.0 collective-permute-done.11.rest_2_
  47.5 0.1 collective-permute-start.15
  47.6 0.0 collective-permute-done.12.rest_3_
  47.6 0.4 collective-permute-start.16
  48.0 2.7 %all-to-all-start.1 = ((f32[32,2,128]{2,1,0:T(2,128)}), f32[32,2,128]{2,1,0:T(2,128)S(1)}, u32[]{:S(2)}, u32[]{:S(2)}) async-start(f32[32,2,128]{2,1,0:T(2,128)} %get-tuple-element.32), calls=%async_computation.1 | async-start | bytes 65536 | tf_op jit(solution)/shard_map/all_to_all | solution.py:502
  50.7 0.0 collective-permute-done.18.rest_2_
  50.7 1.8 %collective-permute-start.17 = (bf16[64,384]{1,0:T(8,128)(2,1)S(1)}, bf16[64,384]{1,0:T(8,128)(2,1)S(1)}, u32[]{:S(2)}, u32[]{:S(2)}) collective-permute-start(bf16[64,384]{1,0:T(8,128)(2,1)S(1)} %get-tuple-element.38.rest_0_), channel_id=1, source_target_pairs={{0,8},{8,0},{16,24},{24,16},{1,9},{9,1},{17,25},{25,17},{2,10},{10... | collective-permute-start | bytes 147464 | tf_op jit(solution)/shard_map/ppermute | solution.py:22
  52.5 2.4 %collective-permute-done.17.rest_1_ = bf16[64,384]{1,0:T(8,128)(2,1)S(1)} collective-permute-done((bf16[64,384]{1,0:T(8,128)(2,1)S(1)}, bf16[64,384]{1,0:T(8,128)(2,1)S(1)}, u32[]{:S(2)}, u32[]{:S(2)}) %collective-permute-start.17) | collective-permute-done | bytes 49184 | tf_op jit(solution)/shard_map/ppermute | solution.py:22
  54.9 1.2 %projgrad.1 = f32[1536,128]{1,0:T(8,128)} custom-call(bf16[64,2048]{1,0:T(8,128)(2,1)S(1)} %copy-done.1, bf16[64,384]{1,0:T(8,128)(2,1)S(1)} %get-tuple-element.38.rest_0_, bf16[64,384]{1,0:T(8,128)(2,1)S(1)} %collective-permute-done.17.rest_1_, bf16[64,384]{1,0:T(8,128)(2,1)S(1)} %collective-permute-done.18.rest_2_, ...), custom_call_target="tpu_custom_call" | custom-call | flops 100663296 | bytes 786432 | tf_op jit(solution)/shard_map/projgrad/pallas_call | solution.py:506
  56.1 1.8 %all-to-all-done.1.sums_ref = f32[32,2,128]{2,1,0:T(2,128)S(1)} async-done(((f32[32,2,128]{2,1,0:T(2,128)}), f32[32,2,128]{2,1,0:T(2,128)S(1)}, u32[]{:S(2)}, u32[]{:S(2)}) %all-to-all-start.1) | async-done | bytes 32800 | tf_op jit(solution)/shard_map/all_to_all | solution.py:502
  57.9 0.0 collective-permute-done.13.rest_4_
  57.9 0.0 collective-permute-done.14.rest_5_
  57.9 0.8 %finish.1 = (bf16[128,1024]{1,0:T(8,128)(2,1)}, f32[2,128]{1,0:T(2,128)}) custom-call(f32[32,2,128]{2,1,0:T(2,128)S(1)} %all-to-all-done.1.sums_ref, bf16[2,128,128]{2,1,0:T(8,128)(2,1)S(1)} %get-tuple-element.33.rest_0_, bf16[2,128,128]{2,1,0:T(8,128)(2,1)S(1)} %collective-permute-done.10.rest_1_, bf16[2,128,128]{2,1,0:T(8,128)(2,1)S(1)} %collective-permute-done.11.rest_2_, ...), custom_call_target="tpu_custom_call" | custom-call | bytes 524288 | tf_op jit(solution)/shard_map/finish/pallas_call | solution.py:515
  (20 shorter events, 0.0 us)
Async XLA Ops:
  0.6 14.4 %copy-start.4 = (s32[8]{0:T(128)S(1)}, s32[8]{0:T(128)}, u32[]{:S(2)}) copy-start(s32[8]{0:T(128)} %frames_hbm.3) | copy-start | bytes 100
  0.6 14.3 %copy-start.2 = (bf16[1,128,64]{1,2,0:T(8,128)(2,1)S(1)}, bf16[1,128,64]{1,2,0:T(8,128)(2,1)}, u32[]{:S(2)}) copy-start(bf16[1,128,64]{1,2,0:T(8,128)(2,1)} %param.17) | copy-start | bytes 49156
  0.7 14.3 %copy-start.7 = (f32[8]{0:T(128)S(1)}, f32[8]{0:T(128)}, u32[]{:S(2)}) copy-start(f32[8]{0:T(128)} %times_hbm.1) | copy-start | bytes 100
  0.7 14.3 %copy-start.6 = (s32[8]{0:T(128)S(1)}, s32[8]{0:T(128)}, u32[]{:S(2)}) copy-start(s32[8]{0:T(128)} %offset_hbm.1) | copy-start | bytes 100
  0.7 14.3 %copy-start.5 = (s32[8]{0:T(128)S(1)}, s32[8]{0:T(128)}, u32[]{:S(2)}) copy-start(s32[8]{0:T(128)} %group_hbm.1) | copy-start | bytes 100
  0.7 27.2 %copy-start.1 = (bf16[64,2048]{1,0:T(8,128)(2,1)S(1)}, bf16[64,2048]{1,0:T(8,128)(2,1)}, u32[]{:S(2)}) copy-start(bf16[64,2048]{1,0:T(8,128)(2,1)} %embed_ref.1) | copy-start | bytes 786436
  0.7 27.2 %copy-start.3 = (f32[2,128]{1,0:T(2,128)S(1)}, f32[2,128]{1,0:T(2,128)}, u32[]{:S(2)}) copy-start(f32[2,128]{1,0:T(2,128)} %gains_hbm.1) | copy-start | bytes 3076
  0.7 27.2 %copy-start = (bf16[2048,3,1,128]{3,0,2,1:T(8,128)(2,1)S(1)}, bf16[2048,3,1,128]{3,0,2,1:T(8,128)(2,1)}, u32[]{:S(2)}) copy-start(bf16[2048,3,1,128]{3,0,2,1:T(8,128)(2,1)} %param.19) | copy-start | bytes 4718596
  2.5 26.3 %all-to-all-start = ((bf16[8,128,128]{2,1,0:T(8,128)(2,1)}), bf16[8,128,128]{2,1,0:T(8,128)(2,1)S(1)}, u32[]{:S(2)}, u32[]{:S(2)}) async-start(bf16[8,128,128]{2,1,0:T(8,128)(2,1)} %split.1), calls=%async_computation | async-start | bytes 524288 | tf_op jit(solution)/shard_map/all_to_all | solution.py:405
  11.4 5.0 %collective-permute-start.2 = (bf16[160,128]{1,0:T(8,128)(2,1)S(1)}, bf16[160,128]{1,0:T(8,128)(2,1)S(1)}, u32[]{:S(2)}, u32[]{:S(2)}) collective-permute-start(bf16[160,128]{1,0:T(8,128)(2,1)S(1)} %conv.1.after_ref.rest_0_), channel_id=1, source_target_pairs={{0,24},{8,16},{16,8},{24,0},{1,25},{9,17},{17,9},{25,1},{2,26},{10... | collective-permute-start | bytes 122888 | tf_op jit(solution)/shard_map/ppermute | solution.py:22
  13.9 4.0 %collective-permute-start.1 = (bf16[160,128]{1,0:T(8,128)(2,1)S(1)}, bf16[160,128]{1,0:T(8,128)(2,1)S(1)}, u32[]{:S(2)}, u32[]{:S(2)}) collective-permute-start(bf16[160,128]{1,0:T(8,128)(2,1)S(1)} %conv.1.after_ref.rest_0_), channel_id=1, source_target_pairs={{0,16},{8,24},{16,0},{24,8},{1,17},{9,25},{17,1},{25,9},{2,18},{10... | collective-permute-start | bytes 122888 | tf_op jit(solution)/shard_map/ppermute | solution.py:22
  14.4 4.0 %collective-permute-start = (bf16[160,128]{1,0:T(8,128)(2,1)S(1)}, bf16[160,128]{1,0:T(8,128)(2,1)S(1)}, u32[]{:S(2)}, u32[]{:S(2)}) collective-permute-start(bf16[160,128]{1,0:T(8,128)(2,1)S(1)} %conv.1.after_ref.rest_0_), channel_id=1, source_target_pairs={{0,8},{8,0},{16,24},{24,16},{1,9},{9,1},{17,25},{25,17},{2,10},{10... | collective-permute-start | bytes 122888 | tf_op jit(solution)/shard_map/ppermute | solution.py:22
  18.7 5.8 %collective-permute-start.8 = (bf16[128,128]{1,0:T(8,128)(2,1)S(1)}, bf16[128,128]{1,0:T(8,128)(2,1)S(1)}, u32[]{:S(2)}, u32[]{:S(2)}) collective-permute-start(bf16[128,128]{1,0:T(8,128)(2,1)S(1)} %get-tuple-element.25.after_ref.rest_0_), channel_id=1, source_target_pairs={{0,6},{1,7},{2,4},{3,5},{4,2},{5,3},{6,0},{7,1},{8,14},{9,15},{10,... | collective-permute-start | bytes 98312 | tf_op jit(solution)/shard_map/ppermute | solution.py:22
  22.5 4.8 %collective-permute-start.6 = (bf16[128,128]{1,0:T(8,128)(2,1)S(1)}, bf16[128,128]{1,0:T(8,128)(2,1)S(1)}, u32[]{:S(2)}, u32[]{:S(2)}) collective-permute-start(bf16[128,128]{1,0:T(8,128)(2,1)S(1)} %get-tuple-element.25.after_ref.rest_0_), channel_id=1, source_target_pairs={{0,4},{1,5},{2,6},{3,7},{4,0},{5,1},{6,2},{7,3},{8,12},{9,13},{10,... | collective-permute-start | bytes 98312 | tf_op jit(solution)/shard_map/ppermute | solution.py:22
  22.5 4.8 %collective-permute-start.4 = (bf16[128,128]{1,0:T(8,128)(2,1)S(1)}, bf16[128,128]{1,0:T(8,128)(2,1)S(1)}, u32[]{:S(2)}, u32[]{:S(2)}) collective-permute-start(bf16[128,128]{1,0:T(8,128)(2,1)S(1)} %get-tuple-element.25.after_ref.rest_0_), channel_id=1, source_target_pairs={{0,2},{1,3},{2,0},{3,1},{4,6},{5,7},{6,4},{7,5},{8,10},{9,11},{10,... | collective-permute-start | bytes 98312 | tf_op jit(solution)/shard_map/ppermute | solution.py:22
  23.2 5.6 %collective-permute-start.3 = (bf16[128,128]{1,0:T(8,128)(2,1)S(1)}, bf16[128,128]{1,0:T(8,128)(2,1)S(1)}, u32[]{:S(2)}, u32[]{:S(2)}) collective-permute-start(bf16[128,128]{1,0:T(8,128)(2,1)S(1)} %get-tuple-element.25.after_ref.rest_0_), channel_id=1, source_target_pairs={{0,1},{1,0},{2,3},{3,2},{4,5},{5,4},{6,7},{7,6},{8,9},{9,8},{10,11... | collective-permute-start | bytes 98312 | tf_op jit(solution)/shard_map/ppermute | solution.py:22
  24.5 4.3 %collective-permute-start.9 = (bf16[128,128]{1,0:T(8,128)(2,1)S(1)}, bf16[128,128]{1,0:T(8,128)(2,1)S(1)}, u32[]{:S(2)}, u32[]{:S(2)}) collective-permute-start(bf16[128,128]{1,0:T(8,128)(2,1)S(1)} %collective-permute-done.8.rest_6_), channel_id=1, source_target_pairs={{0,1},{1,0},{2,3},{3,2},{4,5},{5,4},{6,7},{7,6},{8,9},{9,8},{10,11... | collective-permute-start | bytes 98312 | tf_op jit(solution)/shard_map/ppermute | solution.py:22
  27.4 1.4 %collective-permute-start.7 = (bf16[128,128]{1,0:T(8,128)(2,1)S(1)}, bf16[128,128]{1,0:T(8,128)(2,1)S(1)}, u32[]{:S(2)}, u32[]{:S(2)}) collective-permute-start(bf16[128,128]{1,0:T(8,128)(2,1)S(1)} %collective-permute-done.6.rest_4_), channel_id=1, source_target_pairs={{0,1},{1,0},{2,3},{3,2},{4,5},{5,4},{6,7},{7,6},{8,9},{9,8},{10,11... | collective-permute-start | bytes 98312 | tf_op jit(solution)/shard_map/ppermute | solution.py:22
  27.4 1.4 %collective-permute-start.5 = (bf16[128,128]{1,0:T(8,128)(2,1)S(1)}, bf16[128,128]{1,0:T(8,128)(2,1)S(1)}, u32[]{:S(2)}, u32[]{:S(2)}) collective-permute-start(bf16[128,128]{1,0:T(8,128)(2,1)S(1)} %collective-permute-done.4.rest_2_), channel_id=1, source_target_pairs={{0,1},{1,0},{2,3},{3,2},{4,5},{5,4},{6,7},{7,6},{8,9},{9,8},{10,11... | collective-permute-start | bytes 98312 | tf_op jit(solution)/shard_map/ppermute | solution.py:22
  37.6 9.4 %collective-permute-start.10 = (bf16[2,128,128]{2,1,0:T(8,128)(2,1)S(1)}, bf16[2,128,128]{2,1,0:T(8,128)(2,1)S(1)}, u32[]{:S(2)}, u32[]{:S(2)}) collective-permute-start(bf16[2,128,128]{2,1,0:T(8,128)(2,1)S(1)} %get-tuple-element.34), channel_id=1, source_target_pairs={{0,2},{1,3},{2,0},{3,1},{4,6},{5,7},{6,4},{7,5},{8,10},{9,11},{10,... | collective-permute-start | bytes 196616 | tf_op jit(solution)/shard_map/ppermute | solution.py:22
  37.6 9.9 %collective-permute-start.11 = (bf16[2,128,128]{2,1,0:T(8,128)(2,1)S(1)}, bf16[2,128,128]{2,1,0:T(8,128)(2,1)S(1)}, u32[]{:S(2)}, u32[]{:S(2)}) collective-permute-start(bf16[2,128,128]{2,1,0:T(8,128)(2,1)S(1)} %get-tuple-element.35), channel_id=1, source_target_pairs={{0,4},{1,5},{2,6},{3,7},{4,0},{5,1},{6,2},{7,3},{8,12},{9,13},{10,... | collective-permute-start | bytes 196616 | tf_op jit(solution)/shard_map/ppermute | solution.py:22
  39.4 8.2 %collective-permute-start.12 = (bf16[2,128,128]{2,1,0:T(8,128)(2,1)S(1)}, bf16[2,128,128]{2,1,0:T(8,128)(2,1)S(1)}, u32[]{:S(2)}, u32[]{:S(2)}) collective-permute-start(bf16[2,128,128]{2,1,0:T(8,128)(2,1)S(1)} %get-tuple-element.36), channel_id=1, source_target_pairs={{0,6},{1,7},{2,4},{3,5},{4,2},{5,3},{6,0},{7,1},{8,14},{9,15},{10,... | collective-permute-start | bytes 196616 | tf_op jit(solution)/shard_map/ppermute | solution.py:22
  42.0 5.0 %collective-permute-start.19 = (bf16[64,384]{1,0:T(8,128)(2,1)S(1)}, bf16[64,384]{1,0:T(8,128)(2,1)S(1)}, u32[]{:S(2)}, u32[]{:S(2)}) collective-permute-start(bf16[64,384]{1,0:T(8,128)(2,1)S(1)} %get-tuple-element.38.rest_0_), channel_id=1, source_target_pairs={{0,24},{8,16},{16,8},{24,0},{1,25},{9,17},{17,9},{25,1},{2,26},{10... | collective-permute-start | bytes 147464 | tf_op jit(solution)/shard_map/ppermute | solution.py:22
  43.5 7.2 %collective-permute-start.18 = (bf16[64,384]{1,0:T(8,128)(2,1)S(1)}, bf16[64,384]{1,0:T(8,128)(2,1)S(1)}, u32[]{:S(2)}, u32[]{:S(2)}) collective-permute-start(bf16[64,384]{1,0:T(8,128)(2,1)S(1)} %get-tuple-element.38.rest_0_), channel_id=1, source_target_pairs={{0,16},{8,24},{16,0},{24,8},{1,17},{9,25},{17,1},{25,9},{2,18},{10... | collective-permute-start | bytes 147464 | tf_op jit(solution)/shard_map/ppermute | solution.py:22
  47.0 10.9 %collective-permute-start.13 = (bf16[2,128,128]{2,1,0:T(8,128)(2,1)S(1)}, bf16[2,128,128]{2,1,0:T(8,128)(2,1)S(1)}, u32[]{:S(2)}, u32[]{:S(2)}) collective-permute-start(bf16[2,128,128]{2,1,0:T(8,128)(2,1)S(1)} %get-tuple-element.33.rest_0_), channel_id=1, source_target_pairs={{0,1},{1,0},{2,3},{3,2},{4,5},{5,4},{6,7},{7,6},{8,9},{9,8},{10,11... | collective-permute-start | bytes 196616 | tf_op jit(solution)/shard_map/ppermute | solution.py:22
  47.0 10.9 %collective-permute-start.14 = (bf16[2,128,128]{2,1,0:T(8,128)(2,1)S(1)}, bf16[2,128,128]{2,1,0:T(8,128)(2,1)S(1)}, u32[]{:S(2)}, u32[]{:S(2)}) collective-permute-start(bf16[2,128,128]{2,1,0:T(8,128)(2,1)S(1)} %collective-permute-done.10.rest_1_), channel_id=1, source_target_pairs={{0,1},{1,0},{2,3},{3,2},{4,5},{5,4},{6,7},{7,6},{8,9},{9,8},{10,11... | collective-permute-start | bytes 196616 | tf_op jit(solution)/shard_map/ppermute | solution.py:22
  47.5 10.4 %collective-permute-start.15 = (bf16[2,128,128]{2,1,0:T(8,128)(2,1)S(1)}, bf16[2,128,128]{2,1,0:T(8,128)(2,1)S(1)}, u32[]{:S(2)}, u32[]{:S(2)}) collective-permute-start(bf16[2,128,128]{2,1,0:T(8,128)(2,1)S(1)} %collective-permute-done.11.rest_2_), channel_id=1, source_target_pairs={{0,1},{1,0},{2,3},{3,2},{4,5},{5,4},{6,7},{7,6},{8,9},{9,8},{10,11... | collective-permute-start | bytes 196616 | tf_op jit(solution)/shard_map/ppermute | solution.py:22
  47.6 10.4 %collective-permute-start.16 = (bf16[2,128,128]{2,1,0:T(8,128)(2,1)S(1)}, bf16[2,128,128]{2,1,0:T(8,128)(2,1)S(1)}, u32[]{:S(2)}, u32[]{:S(2)}) collective-permute-start(bf16[2,128,128]{2,1,0:T(8,128)(2,1)S(1)} %collective-permute-done.12.rest_3_), channel_id=1, source_target_pairs={{0,1},{1,0},{2,3},{3,2},{4,5},{5,4},{6,7},{7,6},{8,9},{9,8},{10,11... | collective-permute-start | bytes 196616 | tf_op jit(solution)/shard_map/ppermute | solution.py:22
  48.0 9.9 %all-to-all-start.1 = ((f32[32,2,128]{2,1,0:T(2,128)}), f32[32,2,128]{2,1,0:T(2,128)S(1)}, u32[]{:S(2)}, u32[]{:S(2)}) async-start(f32[32,2,128]{2,1,0:T(2,128)} %get-tuple-element.32), calls=%async_computation.1 | async-start | bytes 65536 | tf_op jit(solution)/shard_map/all_to_all | solution.py:502
  50.7 4.2 %collective-permute-start.17 = (bf16[64,384]{1,0:T(8,128)(2,1)S(1)}, bf16[64,384]{1,0:T(8,128)(2,1)S(1)}, u32[]{:S(2)}, u32[]{:S(2)}) collective-permute-start(bf16[64,384]{1,0:T(8,128)(2,1)S(1)} %get-tuple-element.38.rest_0_), channel_id=1, source_target_pairs={{0,8},{8,0},{16,24},{24,16},{1,9},{9,1},{17,25},{25,17},{2,10},{10... | collective-permute-start | bytes 147464 | tf_op jit(solution)/shard_map/ppermute | solution.py:22
where the time goes:
time: 59 us; the launch traced here: 58.7 us
  starting transfers between devices  26.9 us (46%)
  Pallas kernels  17.3 us (29%)
  waiting for transfers between devices  13.7 us (23%)
  between operations  0.84 us (1%)
    ppermute x20, starting transfers between devices, swap(): lax.ppermute(block, axis, [(i, i ^ mask) for i in range(lax.axis_size(axi...  17.8 us
    ppermute x20, waiting for transfers between devices, swap(): lax.ppermute(block, axis, [(i, i ^ mask) for i in range(lax.axis_size(axi...  11.9 us
    pallas_call x1, Pallas kernels, body(): pl.pallas_call(functools.partial(attention_kernel, (fr, cols, n_seq, patc...  8.8 us
    all_to_all x1, starting transfers between devices, body(): cots = lax.all_to_all(cots, 'seq', **gather)  6.37 us
    all_to_all x1, starting transfers between devices, body(): gain_all = lax.all_to_all(gain, ('dp', 'seq'), **gather)  2.65 us
    pallas_call x1, Pallas kernels, body(): pl.pallas_call(functools.partial(conv_kernel, (fr, wd, ch, lat, clips)),...  2.56 us
    all_to_all x1, waiting for transfers between devices, body(): gain_all = lax.all_to_all(gain, ('dp', 'seq'), **gather)  1.82 us
    pallas_call x1, Pallas kernels, body(): pl.pallas_call(functools.partial(split_kernel, (n_seq, head)), out_shape=...  1.78 us
  transfers between devices with their start and end apart: 22, of which 8 were waited for; matrix products, arithmetic and copies ran while one was open for 0% of the time, Pallas kernels for 10%

commit v1 on v0

--- a/solution.py
+++ b/solution.py
@@ -13,6 +13,7 @@
 LOG2E = 1.4426950408889634
 EPS = 1e-06
 BIG = 16384.0
+EXTRA = 16
 CELLS = ((0, 0), (0, 1), (1, 0), (1, 1), (2, 0), (2, 1), (-1, 0), (-1, 1))
 NT = (((1,), (1,)), ((), ()))
 TN = (((0,), (0,)), ((), ()))
@@ -38,19 +39,18 @@
 HBM = pl.BlockSpec(memory_space=pltpu.HBM)
 
 
-def split(x):
-    high = x.astype(BF16)
-    return high, (x - high.astype(F32)).astype(BF16)
-
-
-def split_kernel(dims, cot_hbm, cots_ref, sems):
+def split_kernel(dims, cot_hbm, *rest):
     n_seq, head = dims
-    loads = [
-        pltpu.make_async_copy(
-            cot_hbm.at[:, h * head : (h + 1) * head], cots_ref.at[h], sems.at[h]
+    pair_refs, sems = rest[: n_seq // 2], rest[n_seq // 2]
+    me = lax.axis_index("seq")
+    loads = []
+    for m in range(n_seq):
+        at = pl.multiple_of((me ^ m) * head, head)
+        loads.append(
+            pltpu.make_async_copy(
+                cot_hbm.at[:, pl.ds(at, head)], pair_refs[m // 2].at[m % 2], sems.at[m]
+            )
         )
-        for h in range(n_seq)
-    ]
     for load in loads:
         load.start()
     for load in loads:
@@ -223,24 +223,28 @@
     loads[0].wait()
     for i in range(3):
         loads[2 + i].wait()
-        both = jnp.dot(embed_ref[...], proj_ref[i], preferred_element_type=F32)
-        high, low = split(both)
-        out_ref[:patch, i * head : (i + 1) * head] = high
-        out_ref[patch:, i * head : (i + 1) * head] = low
+        both = jnp.dot(embed_ref[...], proj_ref[i], preferred_element_type=F32).astype(BF16)
+        at = slice(i * head, (i + 1) * head)
+        out_ref[:patch, at] = both
+        out_ref[patch : 3 * patch, at] = jnp.zeros((2 * patch, head), BF16)
+        out_ref[3 * patch :, at] = both
     loads[1].wait()
 
 
-def mean_of(values, head):
-    ones = jnp.full((2 * head, head), 1.0 / head, BF16)
-    return jnp.dot(jnp.concatenate(split(values), axis=1), ones, preferred_element_type=F32)
-
-
-def attention_kernel(dims, gains_ref, w_ref, own_ref, live_ref, mark_ref, cots_ref, *rest):
-    fr, cols, n_seq, patch, head, tile, devices = dims
-    tok_refs, rest = rest[:n_seq], rest[n_seq:]
-    noisy_ref, grad_ref, gain_ref = rest[:3]
-    pairs_refs, rest = rest[3 : 3 + n_seq // 2], rest[3 + n_seq // 2 :]
-    tok_ref, toks_ref, x_ref, q_ref, k_ref, v_ref, o_ref, dq_ref, dk_ref, dv_ref = rest
+def mean_of(values):
+    return jnp.mean(values, axis=-1, keepdims=True)
+
+
+def chunk_of(size):
+    return min(size, 512)
+
+
+def attention_kernel(dims, gains_ref, w_ref, own_ref, live_ref, mark_ref, *rest):
+    fr, cols, n_seq, patch, head, tile = dims
+    tok_refs, cot_refs, rest = rest[:n_seq], rest[n_seq : 2 * n_seq], rest[2 * n_seq :]
+    noisy_ref, grad_ref = rest[:2]
+    pairs_refs, rest = rest[2 : 2 + n_seq // 2], rest[2 + n_seq // 2 :]
+    tok_ref, inc_ref, cat_ref, unit_ref, scale_ref, q_ref, k_ref, v_ref, o_ref, dq_ref, dk_ref, dv_ref = rest
     me = lax.axis_index("seq")
     blk = fr * cols
     size = n_seq * blk
@@ -250,6 +254,7 @@
     for m in range(n_seq):
         at = pl.multiple_of((me ^ m) * blk, blk)
         tok_ref[pl.ds(at + blk, blk), :] = tok_refs[m][...]
+        inc_ref[pl.ds(at, blk), :] = cot_refs[m // 2 + (m % 2) * (n_seq // 2)][m % 2]
     own_at = pl.multiple_of(me * blk, blk)
     lane = lax.broadcasted_iota(jnp.int32, (blk, width), 1)
     side = jnp.where(
@@ -259,30 +264,33 @@
     )
     noisy = own_ref[...] + pltpu.roll(side, patch, 1)
     noisy_ref[...] = noisy.T[:patch, :]
+    marks = jnp.concatenate([mark_ref[...].astype(BF16)] * (chunk_of(size) // blk), axis=0)
+    away = ((marks.astype(F32) - 1.0) * BIG).astype(BF16)
     weights = w_ref[...]
-    mark = mark_ref[...]
-    for p in range(n_seq):
-        rows = slice(p * blk, (p + 1) * blk)
-        side = jnp.where(
+    chunk = chunk_of(size)
+    lane = lax.broadcasted_iota(jnp.int32, (chunk, width), 1)
+    for p in range(size // chunk):
+        at = p * chunk
+        rows = slice(at, at + chunk)
+        cat_ref[rows, :width] = tok_ref[at + blk : at + blk + chunk, :]
+        cat_ref[rows, width:] = jnp.where(
             lane < patch + patch // 2,
             tok_ref[rows, :].astype(F32),
-            tok_ref[(p + 2) * blk : (p + 3) * blk, :].astype(F32),
-        )
-        tok = tok_ref[(p + 1) * blk : (p + 2) * blk, :].astype(F32) + pltpu.roll(side, patch, 1)
-        tok = jnp.where(lane < patch, tok, pltpu.roll(tok, patch, 1)).astype(BF16)
-        toks_ref[rows, :] = tok
-        x = jnp.dot(tok, weights, preferred_element_type=F32)
-        x_ref[rows, :] = x
-        scale = lax.rsqrt(mean_of(x[:, :head] * x[:, :head], head) + EPS)
-        gain = gains_ref[0:1, :] * (head**-0.5 * LOG2E)
-        q_ref[rows, :head] = (x[:, :head] * scale * gain).astype(BF16)
-        q_ref[rows, head:] = mark.astype(BF16)
-        x = x[:, head:]
-        scale = lax.rsqrt(mean_of(x[:, :head] * x[:, :head], head) + EPS)
-        k_ref[rows, :head] = (x[:, :head] * scale * gains_ref[1:2, :]).astype(BF16)
-        k_ref[rows, head:] = ((mark - 1.0) * BIG).astype(BF16)
-        v_ref[rows, :head] = x[:, head:].astype(BF16)
-        v_ref[rows, head:] = jnp.ones((blk, head), BF16)
+            tok_ref[at + 2 * blk : at + 2 * blk + chunk, :].astype(F32),
+        ).astype(BF16)
+        x = jnp.dot(cat_ref[rows, :], weights, preferred_element_type=F32)
+        v_ref[rows, :head] = x[:, 2 * head :].astype(BF16)
+        v_ref[rows, head:] = jnp.ones((chunk, head), BF16)
+        for i, ref in enumerate((q_ref, k_ref)):
+            mine = x[:, i * head : (i + 1) * head]
+            scale = jnp.broadcast_to(lax.rsqrt(mean_of(mine * mine) + EPS), mine.shape)
+            unit = mine * scale
+            unit_ref[rows, i * head : (i + 1) * head] = unit
+            scale_ref[rows, i * head : (i + 1) * head] = scale
+            gain = gains_ref[i : i + 1, :] * (1.0 if i else head**-0.5 * LOG2E)
+            ref[rows, :head] = (unit * gain).astype(BF16)
+        q_ref[rows, head:] = marks
+        k_ref[rows, head:] = away
     per = tile // blk
     live = jnp.concatenate([live_ref[...]] * per, axis=0)
     for i in range(size // tile):
@@ -294,8 +302,7 @@
         inverse = 1.0 / both[:, head:]
         output = both[:, :head] * inverse
         o_ref[rows, :] = (output * live).astype(BF16)
-        incoming = cots_ref[i * per : (i + 1) * per].reshape(tile, head)
-        scaled = incoming.astype(F32) * live * inverse
+        scaled = inc_ref[rows, :].astype(F32) * live * inverse
         scaled_bf = scaled.astype(BF16)
         upstream = jnp.concatenate([scaled_bf, (-(scaled * output)).astype(BF16)], axis=1)
         prob_grad = lax.dot_general(upstream, v_ref[...], NT, preferred_element_type=F32)
@@ -310,56 +317,82 @@
             dk_ref[...] += dk
             dv_ref[...] += dv
 
-    gains = []
+    gains = [None, None]
     grad = None
-    for p in range(n_seq):
-        rows = slice(p * blk, (p + 1) * blk)
+    for p in range(size // chunk):
+        rows = slice(p * chunk, (p + 1) * chunk)
         parts = []
         for i, (ref, unit) in enumerate(((dq_ref, head**-0.5), (dk_ref, 1.0 / LOG2E))):
-            x = x_ref[rows, i * head : (i + 1) * head]
+            mine = unit_ref[rows, i * head : (i + 1) * head]
             up = ref[rows, :] * unit
-            scale = lax.rsqrt(mean_of(x * x, head) + EPS)
-            unit_x = x * scale
             gain_up = up * gains_ref[i : i + 1, :]
-            parts.append((scale * (gain_up - unit_x * mean_of(unit_x * gain_up, head))).astype(BF16))
-            add = jnp.sum(up * unit_x, axis=0, keepdims=True)
-            if p == 0:
-                gains.append(add)
-            else:
-                gains[i] = gains[i] + add
+            scale = scale_ref[rows, i * head : (i + 1) * head]
+            parts.append((scale * (gain_up - mine * mean_of(mine * gain_up))).astype(BF16))
+            add = jnp.sum(up * mine, axis=0, keepdims=True)
+            gains[i] = add if p == 0 else gains[i] + add
         parts.append(dv_ref[rows, :].astype(BF16))
         term = lax.dot_general(
-            toks_ref[rows, :], jnp.concatenate(parts, axis=1), TN, preferred_element_type=F32
+            cat_ref[rows, :], jnp.concatenate(parts, axis=1), TN, preferred_element_type=F32
         )
         grad = term if grad is None else grad + term
-    grad_ref[...] = grad[:patch, :].astype(BF16)
-    gain_ref[...] = jnp.broadcast_to(jnp.concatenate(gains, axis=0)[None], (devices, 2, head))
+    grad_ref[:patch, :] = (grad[:patch, :] + grad[3 * patch :, :]).astype(BF16)
+    sums = jnp.concatenate(gains + [jnp.zeros((1, head), F32)], axis=1)
+    high = sums.astype(BF16).astype(F32)
+    grad_ref[patch:, :] = jnp.concatenate(
+        [high, sums - high, jnp.zeros((EXTRA - 2, 3 * head), F32)], axis=0
+    ).astype(BF16)
     for m in range(n_seq):
         at = pl.multiple_of((me ^ m) * blk, blk)
         pairs_refs[m // 2][m % 2] = o_ref[pl.ds(at, blk), :]
 
 
 def proj_kernel(dims, embed_ref, *rest):
-    n_dp, _, head, rows = dims
+    n_dp, patch, head, rows = dims
     grad_refs, (out_ref,) = rest[:n_dp], rest[n_dp:]
     slab = lax.axis_index("dp")
     part = embed_ref[:, pl.ds(pl.multiple_of(slab * rows, rows), rows)]
     left = jnp.concatenate([part] * n_dp, axis=0)
-    right = jnp.concatenate([ref[...] for ref in grad_refs], axis=0)
+    right = jnp.concatenate([ref[:patch, :] for ref in grad_refs], axis=0)
     result = lax.dot_general(left, right, TN, preferred_element_type=F32)
     for i in range(3):
         out_ref[pl.ds(i, rows, stride=3), :] = result[:, i * head : (i + 1) * head]
 
 
-def finish_kernel(dims, sums_ref, *rest):
+def group_sum_kernel(dims, *rest):
+    n_dp, patch, head = dims
+    grad_refs, (out_ref, all_ref) = rest[:n_dp], rest[n_dp:]
+    slab = lax.axis_index("dp")
+    for m in range(n_dp):
+        all_ref[slab ^ m] = grad_refs[m][patch:, :].astype(F32)
+    total = all_ref[0]
+    for g in range(1, n_dp):
+        total = total + all_ref[g]
+    both = total[0:1, :] + total[1:2, :]
+    out_ref[...] = jnp.concatenate(
+        [both[:, :head], both[:, head : 2 * head], jnp.zeros((6, head), F32)], axis=0
+    )
+
+
+def chip_sum_kernel(dims, *rest):
+    (half,) = dims
+    sum_refs, (out_ref, all_ref) = rest[:half], rest[half:]
+    chip = lax.axis_index("seq") // 2
+    for m in range(half):
+        all_ref[chip ^ m] = sum_refs[m][...]
+    total = all_ref[0]
+    for z in range(1, half):
+        total = total + all_ref[z]
+    out_ref[...] = total
+
+
+def finish_kernel(dims, sum_ref, other_ref, *rest):
     n_seq, head = dims
-    own_refs, other_refs, (out_ref, gain_ref) = rest[: n_seq // 2], rest[n_seq // 2 : n_seq], rest[n_seq:]
+    pair_refs, (out_ref, gain_ref) = rest[:n_seq], rest[n_seq:]
     me = lax.axis_index("seq")
     for m in range(n_seq):
         at = pl.multiple_of((me ^ m) * head, head)
-        source = other_refs if m % 2 else own_refs
-        out_ref[:, pl.ds(at, head)] = source[m // 2][m % 2]
-    gain_ref[...] = jnp.sum(sums_ref[...], axis=0)
+        out_ref[:, pl.ds(at, head)] = pair_refs[m // 2 + (m % 2) * (n_seq // 2)][m % 2]
+    gain_ref[...] = sum_ref[0:2, :] + other_ref[0:2, :]
 
 
 def body(
@@ -388,21 +421,21 @@
     S = jax.ShapeDtypeStruct
 
     rows_out = (fr + 2) * cols
-    tile = min(256, size)
-    devices = n_dp * n_seq
-    gather = dict(split_axis=0, concat_axis=0, tiled=True)
-
+    tile = min(512, size)
+
+    half = n_seq // 2
     cots = pl.pallas_call(
         functools.partial(split_kernel, (n_seq, head)),
-        out_shape=S((n_seq, blk, head), BF16),
+        out_shape=[S((2, blk, head), BF16)] * half,
         in_specs=[HBM],
-        out_specs=VMEM,
+        out_specs=[VMEM] * half,
         scratch_shapes=[pltpu.SemaphoreType.DMA((n_seq,))],
         compiler_params=params(),
         cost_estimate=cost(0, 4 * blk * n_seq * head),
         name="split",
     )(*keep_in(pltpu.HBM, cotangent.reshape(blk, n_seq * head)))
-    cots = lax.all_to_all(cots, "seq", **gather)
+    cots = [cots[0]] + [swap(cots[m], "seq", 2 * m) for m in range(1, half)]
+    cots += [swap(pair, "seq", 1) for pair in cots]
 
     partial = pl.pallas_call(
         functools.partial(conv_kernel, (fr, wd, ch, lat, clips)),
@@ -461,7 +494,7 @@
         toks[m + 1] = swap(toks[m], "seq", 1)
     weights, gains = pl.pallas_call(
         functools.partial(weight_kernel, (patch, head)),
-        out_shape=[S((2 * patch, 3 * head), BF16), S((2, head), F32)],
+        out_shape=[S((4 * patch, 3 * head), BF16), S((2, head), F32)],
         in_specs=[VMEM] + [HBM] * 3,
         out_specs=[VMEM] * 2,
         scratch_shapes=[
@@ -475,16 +508,18 @@
     )(send, embed_weight, attention_proj.transpose(1, 2, 0, 3).reshape(3, model, head), norm_gains)
 
     wide = 2 * head
-    noisy, grad, gain, *pairs = pl.pallas_call(
-        functools.partial(attention_kernel, (fr, cols, n_seq, patch, head, tile, devices)),
-        out_shape=[S((patch, blk), F32), S((patch, 3 * head), BF16), S((devices, 2, head), F32)]
-        + [S((2, blk, head), BF16)] * (n_seq // 2),
-        in_specs=[VMEM] * (6 + n_seq),
-        out_specs=[VMEM] * (3 + n_seq // 2),
+    noisy, grad, *pairs = pl.pallas_call(
+        functools.partial(attention_kernel, (fr, cols, n_seq, patch, head, tile)),
+        out_shape=[S((patch, blk), F32), S((patch + EXTRA, 3 * head), BF16)]
+        + [S((2, blk, head), BF16)] * half,
+        in_specs=[VMEM] * (5 + 2 * n_seq),
+        out_specs=[VMEM] * (2 + half),
         scratch_shapes=[
             pltpu.VMEM((size + 2 * blk, lanes), BF16),
-            pltpu.VMEM((size, lanes), BF16),
-            pltpu.VMEM((size, 3 * head), F32),
+            pltpu.VMEM((size, head), BF16),
+            pltpu.VMEM((size, 2 * lanes), BF16),
+            pltpu.VMEM((size, wide), F32),
+            pltpu.VMEM((size, wide), F32),
             pltpu.VMEM((size, wide), BF16),
             pltpu.VMEM((size, wide), BF16),
             pltpu.VMEM((size, wide), BF16),
@@ -496,12 +531,33 @@
         compiler_params=params(),
         cost_estimate=cost(12 * size * size * head, 2**21, size * size),
         name="attention",
-    )(gains, weights, own, live, mark, cots, *toks)
-
+    )(gains, weights, own, live, mark, *toks, *cots)
+
+    pairs = [pairs[0]] + [swap(pairs[m], "seq", 2 * m) for m in range(1, half)]
     grads = [grad] + [swap(grad, "dp", m) for m in range(1, n_dp)]
-    gain_all = lax.all_to_all(gain, ("dp", "seq"), **gather)
-    pairs = [pairs[0]] + [swap(pairs[m], "seq", 2 * m) for m in range(1, n_seq // 2)]
-    others = [swap(pair, "seq", 1) for pair in pairs]
+    gain = pl.pallas_call(
+        functools.partial(group_sum_kernel, (n_dp, patch, head)),
+        out_shape=S((8, head), F32),
+        in_specs=[VMEM] * n_dp,
+        out_specs=VMEM,
+        scratch_shapes=[pltpu.VMEM((n_dp, EXTRA, 3 * head), F32)],
+        compiler_params=params(),
+        cost_estimate=cost(0, 2**12),
+        name="groupsum",
+    )(*grads)
+    gain = [gain] + [swap(gain, "seq", 2 * m) for m in range(1, half)]
+    gain = pl.pallas_call(
+        functools.partial(chip_sum_kernel, (half,)),
+        out_shape=S((8, head), F32),
+        in_specs=[VMEM] * half,
+        out_specs=VMEM,
+        scratch_shapes=[pltpu.VMEM((half, 8, head), F32)],
+        compiler_params=params(),
+        cost_estimate=cost(0, 2**12),
+        name="chipsum",
+    )(*gain)
+    other = swap(gain, "seq", 1)
+    pairs += [swap(pair, "seq", 1) for pair in pairs]
     rows = model // n_dp
     proj_grad = pl.pallas_call(
         functools.partial(proj_kernel, (n_dp, patch, head, rows)),
@@ -515,12 +571,12 @@
     out, norm_grad = pl.pallas_call(
         functools.partial(finish_kernel, (n_seq, head)),
         out_shape=[S((blk, n_seq * head), BF16), S((2, head), F32)],
-        in_specs=[VMEM] * (1 + n_seq),
+        in_specs=[VMEM] * (2 + n_seq),
         out_specs=[VMEM] * 2,
         compiler_params=params(),
         cost_estimate=cost(0, 4 * blk * n_seq * head),
         name="finish",
-    )(gain_all, *pairs, *others)
+    )(gain, other, *pairs)
     return (
         noisy.T[None],
         out[None],

time: 59 us -> 59.4 us (level)
  waiting for transfers between devices: 13.7 us -> 18.4 us
  Pallas kernels: 17.3 us -> 13.5 us
    all_to_all x2 -> x0, starting transfers between devices: 9.02 us -> none  [the longest x1 6.37 us: body(): cots = lax.all_to_all(cots, 'seq', **gather)]
    ppermute x20 -> x31, starting transfers between devices: 17.8 us -> 26.4 us  [swap(): lax.ppermute(block, axis, [(i, i ^ mask) for i in range(lax.axis_size(axi...]
    ppermute x20 -> x31, waiting for transfers between devices: 11.9 us -> 18.4 us  [swap(): lax.ppermute(block, axis, [(i, i ^ mask) for i in range(lax.axis_size(axi...]
    pallas_call x1, Pallas kernels: 8.8 us -> 5.68 us  [body(): pl.pallas_call(functools.partial(attention_kernel, (fr, cols, n_seq, patc...]
    all_to_all x2 -> x0, waiting for transfers between devices: 1.82 us -> none  [the longest x1 1.82 us: body(): gain_all = lax.all_to_all(gain, ('dp', 'seq'), **gather)]
    pallas_call x1, Pallas kernels: 1.78 us -> 0.94 us  [body(): pl.pallas_call(functools.partial(split_kernel, (n_seq, head)), out_shape=...]
  transfers between devices with their start and end apart: 22 -> 31, of which waited for: 8 -> 7; matrix products, arithmetic and copies ran while one was open for 0% -> 0% of each run, Pallas kernels for 10% -> 7%
where the time goes in v1:
time: 59.4 us; the launch traced here: 59.2 us
  starting transfers between devices  26.4 us (44%)
  waiting for transfers between devices  18.4 us (31%)
  Pallas kernels  13.5 us (23%)
  between operations  0.89 us (1%)
    ppermute x31, starting transfers between devices, swap(): lax.ppermute(block, axis, [(i, i ^ mask) for i in range(lax.axis_size(axi...  26.4 us
    ppermute x31, waiting for transfers between devices, swap(): lax.ppermute(block, axis, [(i, i ^ mask) for i in range(lax.axis_size(axi...  18.4 us
    pallas_call x1, Pallas kernels, body(): pl.pallas_call(functools.partial(attention_kernel, (fr, cols, n_seq, patc...  5.68 us
    pallas_call x1, Pallas kernels, body(): pl.pallas_call(functools.partial(conv_kernel, (fr, wd, ch, lat, clips)),...  2.7 us
    pallas_call x1, Pallas kernels, body(): pl.pallas_call(functools.partial(proj_kernel, (n_dp, patch, head, rows)),...  1.22 us
  transfers between devices with their start and end apart: 31, of which 7 were waited for; matrix products, arithmetic and copies ran while one was open for 0% of the time, Pallas kernels for 7%

profile of v1, /device:TPU:0, one launch (start us, length us, event | category | flops | bytes accessed | tf_op | source)
XLA Modules:
  0.0 59.2 jit_solution(16180481402863114024)
XLA Ops:
  0.7 2.7 %conv.1.after_ref.rest_0_ = bf16[160,128]{1,0:T(8,128)(2,1)S(1)} custom-call(s32[8]{0:T(128)} %frames_hbm.3, bf16[512,512]{1,0:T(8,128)(2,1)} %bitcast.20, bf16[432,512]{1,0:T(8,128)(2,1)} %bitcast.21), custom_call_target="tpu_custom_call" | custom-call | flops 402653184 | bytes 2097152 | tf_op jit(solution)/shard_map/conv/pallas_call | solution.py:440
  3.4 4.0 %collective-permute-start.2 = (bf16[160,128]{1,0:T(8,128)(2,1)S(1)}, bf16[160,128]{1,0:T(8,128)(2,1)S(1)}, u32[]{:S(2)}, u32[]{:S(2)}) collective-permute-start(bf16[160,128]{1,0:T(8,128)(2,1)S(1)} %conv.1.after_ref.rest_0_), channel_id=1, source_target_pairs={{0,24},{8,16},{16,8},{24,0},{1,25},{9,17},{17,9},{25,1},{2,26},{10... | collective-permute-start | bytes 122888 | tf_op jit(solution)/shard_map/ppermute | solution.py:23
  7.4 0.5 collective-permute-start.1
  7.9 0.9 %split.1 = (bf16[2,128,128]{2,1,0:T(8,128)(2,1)S(1)}, bf16[2,128,128]{2,1,0:T(8,128)(2,1)S(1)}, bf16[2,128,128]{2,1,0:T(8,128)(2,1)S(1)}, bf16[2,128,128]{2,1,0:T(8,128)(2,1)S(1)}) custom-call(bf16[128,1024]{1,0:T(8,128)(2,1)} %bitcast.19), custom_call_target="tpu_custom_call" | custom-call | bytes 524288 | tf_op jit(solution)/shard_map/split/pallas_call | solution.py:427
  8.9 1.6 %collective-permute-start.10 = (bf16[2,128,128]{2,1,0:T(8,128)(2,1)S(1)}, bf16[2,128,128]{2,1,0:T(8,128)(2,1)S(1)}, u32[]{:S(2)}, u32[]{:S(2)}) collective-permute-start(bf16[2,128,128]{2,1,0:T(8,128)(2,1)S(1)} %get-tuple-element.35), channel_id=1, source_target_pairs={{0,2},{1,3},{2,0},{3,1},{4,6},{5,7},{6,4},{7,5},{8,10},{9,11},{10,... | collective-permute-start | bytes 196616 | tf_op jit(solution)/shard_map/ppermute | solution.py:23
  10.5 2.6 %collective-permute-start.11 = (bf16[2,128,128]{2,1,0:T(8,128)(2,1)S(1)}, bf16[2,128,128]{2,1,0:T(8,128)(2,1)S(1)}, u32[]{:S(2)}, u32[]{:S(2)}) collective-permute-start(bf16[2,128,128]{2,1,0:T(8,128)(2,1)S(1)} %get-tuple-element.36), channel_id=1, source_target_pairs={{0,4},{1,5},{2,6},{3,7},{4,0},{5,1},{6,2},{7,3},{8,12},{9,13},{10,... | collective-permute-start | bytes 196616 | tf_op jit(solution)/shard_map/ppermute | solution.py:23
  13.1 0.5 collective-permute-start
  13.6 0.0 collective-permute-done.2.rest_3_
  13.6 0.0 collective-permute-start.12
  13.6 0.0 collective-permute-done.1.rest_2_
  13.6 0.1 collective-permute-start.13
  13.8 1.1 %tables.1 = (bf16[128,640]{1,0:T(8,128)(2,1)S(1)}, f32[128,128]{1,0:T(8,128)S(1)}, f32[128,128]{1,0:T(8,128)S(1)}, f32[128,128]{1,0:T(8,128)S(1)}, f32[128,128]{1,0:T(8,128)S(1)}) custom-call(bf16[160,128]{1,0:T(8,128)(2,1)S(1)} %conv.1.after_ref.rest_0_, s32[8]{0:T(128)S(1)} %copy-done.4, s32[8]{0:T(128)S(1)} %copy-done.5, s32[8]{0:T(128)S(1)} %copy-done.6, ...), custom_call_target="tpu_custom_call" | custom-call | flops 4194304 | bytes 2097152 | tf_op jit(solution)/shard_map/tables/pallas_call | solution.py:465
  14.9 2.2 %collective-permute-done.rest_1_ = bf16[160,128]{1,0:T(8,128)(2,1)S(1)} collective-permute-done((bf16[160,128]{1,0:T(8,128)(2,1)S(1)}, bf16[160,128]{1,0:T(8,128)(2,1)S(1)}, u32[]{:S(2)}, u32[]{:S(2)}) %collective-permute-start) | collective-permute-done | bytes 40992 | tf_op jit(solution)/shard_map/ppermute | solution.py:23
  17.1 0.2 slots.1
  17.3 1.6 %collective-permute-start.8 = (bf16[128,128]{1,0:T(8,128)(2,1)S(1)}, bf16[128,128]{1,0:T(8,128)(2,1)S(1)}, u32[]{:S(2)}, u32[]{:S(2)}) collective-permute-start(bf16[128,128]{1,0:T(8,128)(2,1)S(1)} %get-tuple-element.28.after_ref.rest_0_), channel_id=1, source_target_pairs={{0,6},{1,7},{2,4},{3,5},{4,2},{5,3},{6,0},{7,1},{8,14},{9,15},{10,... | collective-permute-start | bytes 98312 | tf_op jit(solution)/shard_map/ppermute | solution.py:23
  18.9 0.3 collective-permute-start.6
  19.3 0.0 collective-permute-done.11.rest_10_
  19.3 2.5 %collective-permute-start.4 = (bf16[128,128]{1,0:T(8,128)(2,1)S(1)}, bf16[128,128]{1,0:T(8,128)(2,1)S(1)}, u32[]{:S(2)}, u32[]{:S(2)}) collective-permute-start(bf16[128,128]{1,0:T(8,128)(2,1)S(1)} %get-tuple-element.28.after_ref.rest_0_), channel_id=1, source_target_pairs={{0,2},{1,3},{2,0},{3,1},{4,6},{5,7},{6,4},{7,5},{8,10},{9,11},{10,... | collective-permute-start | bytes 98312 | tf_op jit(solution)/shard_map/ppermute | solution.py:23
  21.8 0.5 collective-permute-start.14
  22.3 0.9 %collective-permute-done.8.rest_6_ = bf16[128,128]{1,0:T(8,128)(2,1)S(1)} collective-permute-done((bf16[128,128]{1,0:T(8,128)(2,1)S(1)}, bf16[128,128]{1,0:T(8,128)(2,1)S(1)}, u32[]{:S(2)}, u32[]{:S(2)}) %collective-permute-start.8) | collective-permute-done | bytes 32800 | tf_op jit(solution)/shard_map/ppermute | solution.py:23
  23.2 0.9 %collective-permute-done.6.rest_4_ = bf16[128,128]{1,0:T(8,128)(2,1)S(1)} collective-permute-done((bf16[128,128]{1,0:T(8,128)(2,1)S(1)}, bf16[128,128]{1,0:T(8,128)(2,1)S(1)}, u32[]{:S(2)}, u32[]{:S(2)}) %collective-permute-start.6) | collective-permute-done | bytes 32800 | tf_op jit(solution)/shard_map/ppermute | solution.py:23
  24.1 0.0 collective-permute-start.15
  24.1 0.0 collective-permute-done.4.rest_2_
  24.2 0.5 collective-permute-start.16
  24.6 0.0 collective-permute-done.3.rest_1_
  24.6 0.1 collective-permute-start.7
  24.7 0.0 collective-permute-done.9.rest_7_
  24.7 0.4 collective-permute-start.5
  25.2 0.8 %weights.1 = (bf16[256,384]{1,0:T(8,128)(2,1)S(1)}, f32[2,128]{1,0:T(2,128)S(1)}) custom-call(bf16[128,128]{1,0:T(8,128)(2,1)S(1)} %get-tuple-element.28.after_ref.rest_0_, bf16[64,2048]{1,0:T(8,128)(2,1)S(1)} %copy-done.1, bf16[3,2048,128]{2,1,0:T(8,128)(2,1)S(1)} %bitcast.16, f32[2,128]{1,0:T(2,128)S(1)} %copy-done.3), custom_call_target="tpu_custom_call" | custom-call | flops 100663296 | bytes 1835008 | tf_op jit(solution)/shard_map/weights/pallas_call | solution.py:495
  26.0 0.0 collective-permute-done.7.rest_5_
  26.1 5.7 %attention.1 = (f32[64,128]{1,0:T(8,128)}, bf16[80,384]{1,0:T(8,128)(2,1)S(1)}, bf16[2,128,128]{2,1,0:T(8,128)(2,1)S(1)}, bf16[2,128,128]{2,1,0:T(8,128)(2,1)S(1...) custom-call(f32[2,128]{1,0:T(2,128)S(1)} %get-tuple-element.29.gains_ref, ...), custom_call_target="tpu_custom_call" | custom-call | flops 1610612736 | bytes 2097152 | tf_op jit(solution)/shard_map/attention/pallas_call | solution.py:511
  31.8 2.0 %collective-permute-start.19 = (bf16[80,384]{1,0:T(8,128)(2,1)S(1)}, bf16[80,384]{1,0:T(8,128)(2,1)S(1)}, u32[]{:S(2)}, u32[]{:S(2)}) collective-permute-start(bf16[80,384]{1,0:T(8,128)(2,1)S(1)} %get-tuple-element.39.rest_0_), channel_id=1, source_target_pairs={{0,24},{8,16},{16,8},{24,0},{1,25},{9,17},{17,9},{25,1},{2,26},{10... | collective-permute-start | bytes 184328 | tf_op jit(solution)/shard_map/ppermute | solution.py:23
  33.8 0.8 %collective-permute-start.24 = (bf16[2,128,128]{2,1,0:T(8,128)(2,1)S(1)}, bf16[2,128,128]{2,1,0:T(8,128)(2,1)S(1)}, u32[]{:S(2)}, u32[]{:S(2)}) collective-permute-start(bf16[2,128,128]{2,1,0:T(8,128)(2,1)S(1)} %get-tuple-element.41), channel_id=1, source_target_pairs={{0,2},{1,3},{2,0},{3,1},{4,6},{5,7},{6,4},{7,5},{8,10},{9,11},{10,... | collective-permute-start | bytes 196616 | tf_op jit(solution)/shard_map/ppermute | solution.py:23
  34.6 1.5 %collective-permute-start.25 = (bf16[2,128,128]{2,1,0:T(8,128)(2,1)S(1)}, bf16[2,128,128]{2,1,0:T(8,128)(2,1)S(1)}, u32[]{:S(2)}, u32[]{:S(2)}) collective-permute-start(bf16[2,128,128]{2,1,0:T(8,128)(2,1)S(1)} %get-tuple-element.42), channel_id=1, source_target_pairs={{0,4},{1,5},{2,6},{3,7},{4,0},{5,1},{6,2},{7,3},{8,12},{9,13},{10,... | collective-permute-start | bytes 196616 | tf_op jit(solution)/shard_map/ppermute | solution.py:23
  36.1 2.1 %collective-permute-start.26 = (bf16[2,128,128]{2,1,0:T(8,128)(2,1)S(1)}, bf16[2,128,128]{2,1,0:T(8,128)(2,1)S(1)}, u32[]{:S(2)}, u32[]{:S(2)}) collective-permute-start(bf16[2,128,128]{2,1,0:T(8,128)(2,1)S(1)} %get-tuple-element.43), channel_id=1, source_target_pairs={{0,6},{1,7},{2,4},{3,5},{4,2},{5,3},{6,0},{7,1},{8,14},{9,15},{10,... | collective-permute-start | bytes 196616 | tf_op jit(solution)/shard_map/ppermute | solution.py:23
  38.2 0.5 collective-permute-start.18
  38.7 0.9 %collective-permute-start.17 = (bf16[80,384]{1,0:T(8,128)(2,1)S(1)}, bf16[80,384]{1,0:T(8,128)(2,1)S(1)}, u32[]{:S(2)}, u32[]{:S(2)}) collective-permute-start(bf16[80,384]{1,0:T(8,128)(2,1)S(1)} %get-tuple-element.39.rest_0_), channel_id=1, source_target_pairs={{0,8},{8,0},{16,24},{24,16},{1,9},{9,1},{17,25},{25,17},{2,10},{10... | collective-permute-start | bytes 184328 | tf_op jit(solution)/shard_map/ppermute | solution.py:23
  39.6 2.8 %collective-permute-done.18.rest_2_ = bf16[80,384]{1,0:T(8,128)(2,1)S(1)} collective-permute-done((bf16[80,384]{1,0:T(8,128)(2,1)S(1)}, bf16[80,384]{1,0:T(8,128)(2,1)S(1)}, u32[]{:S(2)}, u32[]{:S(2)}) %collective-permute-start.18) | collective-permute-done | bytes 61472 | tf_op jit(solution)/shard_map/ppermute | solution.py:23
  42.4 0.5 collective-permute-start.28
  42.9 0.1 collective-permute-start.29
  43.0 0.4 collective-permute-start.30
  43.5 2.1 %collective-permute-start.22 = (f32[8,128]{1,0:T(8,128)S(1)}, f32[8,128]{1,0:T(8,128)S(1)}, u32[]{:S(2)}, u32[]{:S(2)}) collective-permute-start(f32[8,128]{1,0:T(8,128)S(1)} %groupsum.1.rest_0_), channel_id=1, source_target_pairs={{0,6},{1,7},{2,4},{3,5},{4,2},{5,3},{6,0},{7,1},{8,14},{9,15},{10,... | collective-permute-start | bytes 12296 | tf_op jit(solution)/shard_map/ppermute | solution.py:23
  45.6 3.4 %collective-permute-done.22.rest_3_ = f32[8,128]{1,0:T(8,128)S(1)} collective-permute-done((f32[8,128]{1,0:T(8,128)S(1)}, f32[8,128]{1,0:T(8,128)S(1)}, u32[]{:S(2)}, u32[]{:S(2)}) %collective-permute-start.22) | collective-permute-done | bytes 4128 | tf_op jit(solution)/shard_map/ppermute | solution.py:23
  49.0 4.5 %collective-permute-done.21.rest_2_ = f32[8,128]{1,0:T(8,128)S(1)} collective-permute-done((f32[8,128]{1,0:T(8,128)S(1)}, f32[8,128]{1,0:T(8,128)S(1)}, u32[]{:S(2)}, u32[]{:S(2)}) %collective-permute-start.21) | collective-permute-done | bytes 4128 | tf_op jit(solution)/shard_map/ppermute | solution.py:23
  53.5 3.6 %collective-permute-done.20.rest_1_ = f32[8,128]{1,0:T(8,128)S(1)} collective-permute-done((f32[8,128]{1,0:T(8,128)S(1)}, f32[8,128]{1,0:T(8,128)S(1)}, u32[]{:S(2)}, u32[]{:S(2)}) %collective-permute-start.20) | collective-permute-done | bytes 4128 | tf_op jit(solution)/shard_map/ppermute | solution.py:23
  57.1 0.1 collective-permute-start.23
  57.2 1.2 %projgrad.1 = f32[1536,128]{1,0:T(8,128)} custom-call(bf16[64,2048]{1,0:T(8,128)(2,1)S(1)} %copy-done.1, bf16[80,384]{1,0:T(8,128)(2,1)S(1)} %get-tuple-element.39.rest_0_, bf16[80,384]{1,0:T(8,128)(2,1)S(1)} %collective-permute-done.17.rest_1_, bf16[80,384]{1,0:T(8,128)(2,1)S(1)} %collective-permute-done.18.rest_2_, ...), custom_call_target="tpu_custom_call" | custom-call | flops 100663296 | bytes 786432 | tf_op jit(solution)/shard_map/projgrad/pallas_call | solution.py:562
  58.4 0.8 %finish.1 = (bf16[128,1024]{1,0:T(8,128)(2,1)}, f32[2,128]{1,0:T(2,128)}) custom-call(f32[8,128]{1,0:T(8,128)S(1)} %chipsum.1.sum_ref, f32[8,128]{1,0:T(8,128)S(1)} %collective-permute-done.23.other_ref, bf16[2,128,128]{2,1,0:T(8,128)(2,1)S(1)} %get-tuple-element.40.rest_0_, bf16[2,128,128]{2,1,0:T(8,128)(2,1)S(1)} %collective-permute-done.24.rest_1_, ...), custom_call_target="tpu_custom_call" | custom-call | bytes 524288 | tf_op jit(solution)/shard_map/finish/pallas_call | solution.py:571
  (40 shorter events, 0.1 us)
Async XLA Ops:
  0.6 13.1 %copy-start.4 = (s32[8]{0:T(128)S(1)}, s32[8]{0:T(128)}, u32[]{:S(2)}) copy-start(s32[8]{0:T(128)} %frames_hbm.3) | copy-start | bytes 100
  0.6 13.1 %copy-start.2 = (bf16[1,128,64]{1,2,0:T(8,128)(2,1)S(1)}, bf16[1,128,64]{1,2,0:T(8,128)(2,1)}, u32[]{:S(2)}) copy-start(bf16[1,128,64]{1,2,0:T(8,128)(2,1)} %param.17) | copy-start | bytes 49156
  0.7 13.1 %copy-start.7 = (f32[8]{0:T(128)S(1)}, f32[8]{0:T(128)}, u32[]{:S(2)}) copy-start(f32[8]{0:T(128)} %times_hbm.1) | copy-start | bytes 100
  0.7 13.1 %copy-start.6 = (s32[8]{0:T(128)S(1)}, s32[8]{0:T(128)}, u32[]{:S(2)}) copy-start(s32[8]{0:T(128)} %offset_hbm.1) | copy-start | bytes 100
  0.7 13.1 %copy-start.5 = (s32[8]{0:T(128)S(1)}, s32[8]{0:T(128)}, u32[]{:S(2)}) copy-start(s32[8]{0:T(128)} %group_hbm.1) | copy-start | bytes 100
  0.7 24.5 %copy-start.1 = (bf16[64,2048]{1,0:T(8,128)(2,1)S(1)}, bf16[64,2048]{1,0:T(8,128)(2,1)}, u32[]{:S(2)}) copy-start(bf16[64,2048]{1,0:T(8,128)(2,1)} %embed_ref.1) | copy-start | bytes 786436
  0.7 24.5 %copy-start.3 = (f32[2,128]{1,0:T(2,128)S(1)}, f32[2,128]{1,0:T(2,128)}, u32[]{:S(2)}) copy-start(f32[2,128]{1,0:T(2,128)} %gains_hbm.1) | copy-start | bytes 3076
  0.7 24.5 %copy-start = (bf16[2048,3,1,128]{3,0,2,1:T(8,128)(2,1)S(1)}, bf16[2048,3,1,128]{3,0,2,1:T(8,128)(2,1)}, u32[]{:S(2)}) copy-start(bf16[2048,3,1,128]{3,0,2,1:T(8,128)(2,1)} %param.19) | copy-start | bytes 4718596
  3.4 10.2 %collective-permute-start.2 = (bf16[160,128]{1,0:T(8,128)(2,1)S(1)}, bf16[160,128]{1,0:T(8,128)(2,1)S(1)}, u32[]{:S(2)}, u32[]{:S(2)}) collective-permute-start(bf16[160,128]{1,0:T(8,128)(2,1)S(1)} %conv.1.after_ref.rest_0_), channel_id=1, source_target_pairs={{0,24},{8,16},{16,8},{24,0},{1,25},{9,17},{17,9},{25,1},{2,26},{10... | collective-permute-start | bytes 122888 | tf_op jit(solution)/shard_map/ppermute | solution.py:23
  7.4 6.2 %collective-permute-start.1 = (bf16[160,128]{1,0:T(8,128)(2,1)S(1)}, bf16[160,128]{1,0:T(8,128)(2,1)S(1)}, u32[]{:S(2)}, u32[]{:S(2)}) collective-permute-start(bf16[160,128]{1,0:T(8,128)(2,1)S(1)} %conv.1.after_ref.rest_0_), channel_id=1, source_target_pairs={{0,16},{8,24},{16,0},{24,8},{1,17},{9,25},{17,1},{25,9},{2,18},{10... | collective-permute-start | bytes 122888 | tf_op jit(solution)/shard_map/ppermute | solution.py:23
  8.9 10.1 %collective-permute-start.10 = (bf16[2,128,128]{2,1,0:T(8,128)(2,1)S(1)}, bf16[2,128,128]{2,1,0:T(8,128)(2,1)S(1)}, u32[]{:S(2)}, u32[]{:S(2)}) collective-permute-start(bf16[2,128,128]{2,1,0:T(8,128)(2,1)S(1)} %get-tuple-element.35), channel_id=1, source_target_pairs={{0,2},{1,3},{2,0},{3,1},{4,6},{5,7},{6,4},{7,5},{8,10},{9,11},{10,... | collective-permute-start | bytes 196616 | tf_op jit(solution)/shard_map/ppermute | solution.py:23
  10.5 8.8 %collective-permute-start.11 = (bf16[2,128,128]{2,1,0:T(8,128)(2,1)S(1)}, bf16[2,128,128]{2,1,0:T(8,128)(2,1)S(1)}, u32[]{:S(2)}, u32[]{:S(2)}) collective-permute-start(bf16[2,128,128]{2,1,0:T(8,128)(2,1)S(1)} %get-tuple-element.36), channel_id=1, source_target_pairs={{0,4},{1,5},{2,6},{3,7},{4,0},{5,1},{6,2},{7,3},{8,12},{9,13},{10,... | collective-permute-start | bytes 196616 | tf_op jit(solution)/shard_map/ppermute | solution.py:23
  13.1 4.0 %collective-permute-start = (bf16[160,128]{1,0:T(8,128)(2,1)S(1)}, bf16[160,128]{1,0:T(8,128)(2,1)S(1)}, u32[]{:S(2)}, u32[]{:S(2)}) collective-permute-start(bf16[160,128]{1,0:T(8,128)(2,1)S(1)} %conv.1.after_ref.rest_0_), channel_id=1, source_target_pairs={{0,8},{8,0},{16,24},{24,16},{1,9},{9,1},{17,25},{25,17},{2,10},{10... | collective-permute-start | bytes 122888 | tf_op jit(solution)/shard_map/ppermute | solution.py:23
  13.6 8.1 %collective-permute-start.12 = (bf16[2,128,128]{2,1,0:T(8,128)(2,1)S(1)}, bf16[2,128,128]{2,1,0:T(8,128)(2,1)S(1)}, u32[]{:S(2)}, u32[]{:S(2)}) collective-permute-start(bf16[2,128,128]{2,1,0:T(8,128)(2,1)S(1)} %get-tuple-element.37), channel_id=1, source_target_pairs={{0,6},{1,7},{2,4},{3,5},{4,2},{5,3},{6,0},{7,1},{8,14},{9,15},{10,... | collective-permute-start | bytes 196616 | tf_op jit(solution)/shard_map/ppermute | solution.py:23
  13.6 8.1 %collective-permute-start.13 = (bf16[2,128,128]{2,1,0:T(8,128)(2,1)S(1)}, bf16[2,128,128]{2,1,0:T(8,128)(2,1)S(1)}, u32[]{:S(2)}, u32[]{:S(2)}) collective-permute-start(bf16[2,128,128]{2,1,0:T(8,128)(2,1)S(1)} %get-tuple-element.34.rest_8_), channel_id=1, source_target_pairs={{0,1},{1,0},{2,3},{3,2},{4,5},{5,4},{6,7},{7,6},{8,9},{9,8},{10,11... | collective-permute-start | bytes 196616 | tf_op jit(solution)/shard_map/ppermute | solution.py:23
  17.3 5.9 %collective-permute-start.8 = (bf16[128,128]{1,0:T(8,128)(2,1)S(1)}, bf16[128,128]{1,0:T(8,128)(2,1)S(1)}, u32[]{:S(2)}, u32[]{:S(2)}) collective-permute-start(bf16[128,128]{1,0:T(8,128)(2,1)S(1)} %get-tuple-element.28.after_ref.rest_0_), channel_id=1, source_target_pairs={{0,6},{1,7},{2,4},{3,5},{4,2},{5,3},{6,0},{7,1},{8,14},{9,15},{10,... | collective-permute-start | bytes 98312 | tf_op jit(solution)/shard_map/ppermute | solution.py:23
  18.9 5.2 %collective-permute-start.6 = (bf16[128,128]{1,0:T(8,128)(2,1)S(1)}, bf16[128,128]{1,0:T(8,128)(2,1)S(1)}, u32[]{:S(2)}, u32[]{:S(2)}) collective-permute-start(bf16[128,128]{1,0:T(8,128)(2,1)S(1)} %get-tuple-element.28.after_ref.rest_0_), channel_id=1, source_target_pairs={{0,4},{1,5},{2,6},{3,7},{4,0},{5,1},{6,2},{7,3},{8,12},{9,13},{10,... | collective-permute-start | bytes 98312 | tf_op jit(solution)/shard_map/ppermute | solution.py:23
  19.3 4.9 %collective-permute-start.4 = (bf16[128,128]{1,0:T(8,128)(2,1)S(1)}, bf16[128,128]{1,0:T(8,128)(2,1)S(1)}, u32[]{:S(2)}, u32[]{:S(2)}) collective-permute-start(bf16[128,128]{1,0:T(8,128)(2,1)S(1)} %get-tuple-element.28.after_ref.rest_0_), channel_id=1, source_target_pairs={{0,2},{1,3},{2,0},{3,1},{4,6},{5,7},{6,4},{7,5},{8,10},{9,11},{10,... | collective-permute-start | bytes 98312 | tf_op jit(solution)/shard_map/ppermute | solution.py:23
  21.8 2.9 %collective-permute-start.3 = (bf16[128,128]{1,0:T(8,128)(2,1)S(1)}, bf16[128,128]{1,0:T(8,128)(2,1)S(1)}, u32[]{:S(2)}, u32[]{:S(2)}) collective-permute-start(bf16[128,128]{1,0:T(8,128)(2,1)S(1)} %get-tuple-element.28.after_ref.rest_0_), channel_id=1, source_target_pairs={{0,1},{1,0},{2,3},{3,2},{4,5},{5,4},{6,7},{7,6},{8,9},{9,8},{10,11... | collective-permute-start | bytes 98312 | tf_op jit(solution)/shard_map/ppermute | solution.py:23
  21.8 4.3 %collective-permute-start.14 = (bf16[2,128,128]{2,1,0:T(8,128)(2,1)S(1)}, bf16[2,128,128]{2,1,0:T(8,128)(2,1)S(1)}, u32[]{:S(2)}, u32[]{:S(2)}) collective-permute-start(bf16[2,128,128]{2,1,0:T(8,128)(2,1)S(1)} %collective-permute-done.10.rest_9_), channel_id=1, source_target_pairs={{0,1},{1,0},{2,3},{3,2},{4,5},{5,4},{6,7},{7,6},{8,9},{9,8},{10,11... | collective-permute-start | bytes 196616 | tf_op jit(solution)/shard_map/ppermute | solution.py:23
  23.2 1.5 %collective-permute-start.9 = (bf16[128,128]{1,0:T(8,128)(2,1)S(1)}, bf16[128,128]{1,0:T(8,128)(2,1)S(1)}, u32[]{:S(2)}, u32[]{:S(2)}) collective-permute-start(bf16[128,128]{1,0:T(8,128)(2,1)S(1)} %collective-permute-done.8.rest_6_), channel_id=1, source_target_pairs={{0,1},{1,0},{2,3},{3,2},{4,5},{5,4},{6,7},{7,6},{8,9},{9,8},{10,11... | collective-permute-start | bytes 98312 | tf_op jit(solution)/shard_map/ppermute | solution.py:23
  24.1 1.9 %collective-permute-start.15 = (bf16[2,128,128]{2,1,0:T(8,128)(2,1)S(1)}, bf16[2,128,128]{2,1,0:T(8,128)(2,1)S(1)}, u32[]{:S(2)}, u32[]{:S(2)}) collective-permute-start(bf16[2,128,128]{2,1,0:T(8,128)(2,1)S(1)} %collective-permute-done.11.rest_10_), channel_id=1, source_target_pairs={{0,1},{1,0},{2,3},{3,2},{4,5},{5,4},{6,7},{7,6},{8,9},{9,8},{10,11... | collective-permute-start | bytes 196616 | tf_op jit(solution)/shard_map/ppermute | solution.py:23
  24.2 1.9 %collective-permute-start.16 = (bf16[2,128,128]{2,1,0:T(8,128)(2,1)S(1)}, bf16[2,128,128]{2,1,0:T(8,128)(2,1)S(1)}, u32[]{:S(2)}, u32[]{:S(2)}) collective-permute-start(bf16[2,128,128]{2,1,0:T(8,128)(2,1)S(1)} %collective-permute-done.12.rest_11_), channel_id=1, source_target_pairs={{0,1},{1,0},{2,3},{3,2},{4,5},{5,4},{6,7},{7,6},{8,9},{9,8},{10,11... | collective-permute-start | bytes 196616 | tf_op jit(solution)/shard_map/ppermute | solution.py:23
  24.6 1.4 %collective-permute-start.7 = (bf16[128,128]{1,0:T(8,128)(2,1)S(1)}, bf16[128,128]{1,0:T(8,128)(2,1)S(1)}, u32[]{:S(2)}, u32[]{:S(2)}) collective-permute-start(bf16[128,128]{1,0:T(8,128)(2,1)S(1)} %collective-permute-done.6.rest_4_), channel_id=1, source_target_pairs={{0,1},{1,0},{2,3},{3,2},{4,5},{5,4},{6,7},{7,6},{8,9},{9,8},{10,11... | collective-permute-start | bytes 98312 | tf_op jit(solution)/shard_map/ppermute | solution.py:23
  24.7 1.3 %collective-permute-start.5 = (bf16[128,128]{1,0:T(8,128)(2,1)S(1)}, bf16[128,128]{1,0:T(8,128)(2,1)S(1)}, u32[]{:S(2)}, u32[]{:S(2)}) collective-permute-start(bf16[128,128]{1,0:T(8,128)(2,1)S(1)} %collective-permute-done.4.rest_2_), channel_id=1, source_target_pairs={{0,1},{1,0},{2,3},{3,2},{4,5},{5,4},{6,7},{7,6},{8,9},{9,8},{10,11... | collective-permute-start | bytes 98312 | tf_op jit(solution)/shard_map/ppermute | solution.py:23
  31.8 6.9 %collective-permute-start.19 = (bf16[80,384]{1,0:T(8,128)(2,1)S(1)}, bf16[80,384]{1,0:T(8,128)(2,1)S(1)}, u32[]{:S(2)}, u32[]{:S(2)}) collective-permute-start(bf16[80,384]{1,0:T(8,128)(2,1)S(1)} %get-tuple-element.39.rest_0_), channel_id=1, source_target_pairs={{0,24},{8,16},{16,8},{24,0},{1,25},{9,17},{17,9},{25,1},{2,26},{10... | collective-permute-start | bytes 184328 | tf_op jit(solution)/shard_map/ppermute | solution.py:23
  33.8 8.6 %collective-permute-start.24 = (bf16[2,128,128]{2,1,0:T(8,128)(2,1)S(1)}, bf16[2,128,128]{2,1,0:T(8,128)(2,1)S(1)}, u32[]{:S(2)}, u32[]{:S(2)}) collective-permute-start(bf16[2,128,128]{2,1,0:T(8,128)(2,1)S(1)} %get-tuple-element.41), channel_id=1, source_target_pairs={{0,2},{1,3},{2,0},{3,1},{4,6},{5,7},{6,4},{7,5},{8,10},{9,11},{10,... | collective-permute-start | bytes 196616 | tf_op jit(solution)/shard_map/ppermute | solution.py:23
  34.6 8.3 %collective-permute-start.25 = (bf16[2,128,128]{2,1,0:T(8,128)(2,1)S(1)}, bf16[2,128,128]{2,1,0:T(8,128)(2,1)S(1)}, u32[]{:S(2)}, u32[]{:S(2)}) collective-permute-start(bf16[2,128,128]{2,1,0:T(8,128)(2,1)S(1)} %get-tuple-element.42), channel_id=1, source_target_pairs={{0,4},{1,5},{2,6},{3,7},{4,0},{5,1},{6,2},{7,3},{8,12},{9,13},{10,... | collective-permute-start | bytes 196616 | tf_op jit(solution)/shard_map/ppermute | solution.py:23
  36.1 6.9 %collective-permute-start.26 = (bf16[2,128,128]{2,1,0:T(8,128)(2,1)S(1)}, bf16[2,128,128]{2,1,0:T(8,128)(2,1)S(1)}, u32[]{:S(2)}, u32[]{:S(2)}) collective-permute-start(bf16[2,128,128]{2,1,0:T(8,128)(2,1)S(1)} %get-tuple-element.43), channel_id=1, source_target_pairs={{0,6},{1,7},{2,4},{3,5},{4,2},{5,3},{6,0},{7,1},{8,14},{9,15},{10,... | collective-permute-start | bytes 196616 | tf_op jit(solution)/shard_map/ppermute | solution.py:23
  38.2 4.2 %collective-permute-start.18 = (bf16[80,384]{1,0:T(8,128)(2,1)S(1)}, bf16[80,384]{1,0:T(8,128)(2,1)S(1)}, u32[]{:S(2)}, u32[]{:S(2)}) collective-permute-start(bf16[80,384]{1,0:T(8,128)(2,1)S(1)} %get-tuple-element.39.rest_0_), channel_id=1, source_target_pairs={{0,16},{8,24},{16,0},{24,8},{1,17},{9,25},{17,1},{25,9},{2,18},{10... | collective-permute-start | bytes 184328 | tf_op jit(solution)/shard_map/ppermute | solution.py:23
  38.7 4.7 %collective-permute-start.17 = (bf16[80,384]{1,0:T(8,128)(2,1)S(1)}, bf16[80,384]{1,0:T(8,128)(2,1)S(1)}, u32[]{:S(2)}, u32[]{:S(2)}) collective-permute-start(bf16[80,384]{1,0:T(8,128)(2,1)S(1)} %get-tuple-element.39.rest_0_), channel_id=1, source_target_pairs={{0,8},{8,0},{16,24},{24,16},{1,9},{9,1},{17,25},{25,17},{2,10},{10... | collective-permute-start | bytes 184328 | tf_op jit(solution)/shard_map/ppermute | solution.py:23
  42.4 16.0 %collective-permute-start.27 = (bf16[2,128,128]{2,1,0:T(8,128)(2,1)S(1)}, bf16[2,128,128]{2,1,0:T(8,128)(2,1)S(1)}, u32[]{:S(2)}, u32[]{:S(2)}) collective-permute-start(bf16[2,128,128]{2,1,0:T(8,128)(2,1)S(1)} %get-tuple-element.40.rest_0_), channel_id=1, source_target_pairs={{0,1},{1,0},{2,3},{3,2},{4,5},{5,4},{6,7},{7,6},{8,9},{9,8},{10,11... | collective-permute-start | bytes 196616 | tf_op jit(solution)/shard_map/ppermute | solution.py:23
  42.4 16.0 %collective-permute-start.28 = (bf16[2,128,128]{2,1,0:T(8,128)(2,1)S(1)}, bf16[2,128,128]{2,1,0:T(8,128)(2,1)S(1)}, u32[]{:S(2)}, u32[]{:S(2)}) collective-permute-start(bf16[2,128,128]{2,1,0:T(8,128)(2,1)S(1)} %collective-permute-done.24.rest_1_), channel_id=1, source_target_pairs={{0,1},{1,0},{2,3},{3,2},{4,5},{5,4},{6,7},{7,6},{8,9},{9,8},{10,11... | collective-permute-start | bytes 196616 | tf_op jit(solution)/shard_map/ppermute | solution.py:23
  42.9 15.4 %collective-permute-start.29 = (bf16[2,128,128]{2,1,0:T(8,128)(2,1)S(1)}, bf16[2,128,128]{2,1,0:T(8,128)(2,1)S(1)}, u32[]{:S(2)}, u32[]{:S(2)}) collective-permute-start(bf16[2,128,128]{2,1,0:T(8,128)(2,1)S(1)} %collective-permute-done.25.rest_2_), channel_id=1, source_target_pairs={{0,1},{1,0},{2,3},{3,2},{4,5},{5,4},{6,7},{7,6},{8,9},{9,8},{10,11... | collective-permute-start | bytes 196616 | tf_op jit(solution)/shard_map/ppermute | solution.py:23
  43.0 15.4 %collective-permute-start.30 = (bf16[2,128,128]{2,1,0:T(8,128)(2,1)S(1)}, bf16[2,128,128]{2,1,0:T(8,128)(2,1)S(1)}, u32[]{:S(2)}, u32[]{:S(2)}) collective-permute-start(bf16[2,128,128]{2,1,0:T(8,128)(2,1)S(1)} %collective-permute-done.26.rest_3_), channel_id=1, source_target_pairs={{0,1},{1,0},{2,3},{3,2},{4,5},{5,4},{6,7},{7,6},{8,9},{9,8},{10,11... | collective-permute-start | bytes 196616 | tf_op jit(solution)/shard_map/ppermute | solution.py:23
  43.5 5.5 %collective-permute-start.22 = (f32[8,128]{1,0:T(8,128)S(1)}, f32[8,128]{1,0:T(8,128)S(1)}, u32[]{:S(2)}, u32[]{:S(2)}) collective-permute-start(f32[8,128]{1,0:T(8,128)S(1)} %groupsum.1.rest_0_), channel_id=1, source_target_pairs={{0,6},{1,7},{2,4},{3,5},{4,2},{5,3},{6,0},{7,1},{8,14},{9,15},{10,... | collective-permute-start | bytes 12296 | tf_op jit(solution)/shard_map/ppermute | solution.py:23
  49.0 4.5 %collective-permute-start.21 = (f32[8,128]{1,0:T(8,128)S(1)}, f32[8,128]{1,0:T(8,128)S(1)}, u32[]{:S(2)}, u32[]{:S(2)}) collective-permute-start(f32[8,128]{1,0:T(8,128)S(1)} %groupsum.1.rest_0_), channel_id=1, source_target_pairs={{0,4},{1,5},{2,6},{3,7},{4,0},{5,1},{6,2},{7,3},{8,12},{9,13},{10,... | collective-permute-start | bytes 12296 | tf_op jit(solution)/shard_map/ppermute | solution.py:23
  53.5 3.6 %collective-permute-start.20 = (f32[8,128]{1,0:T(8,128)S(1)}, f32[8,128]{1,0:T(8,128)S(1)}, u32[]{:S(2)}, u32[]{:S(2)}) collective-permute-start(f32[8,128]{1,0:T(8,128)S(1)} %groupsum.1.rest_0_), channel_id=1, source_target_pairs={{0,2},{1,3},{2,0},{3,1},{4,6},{5,7},{6,4},{7,5},{8,10},{9,11},{10,... | collective-permute-start | bytes 12296 | tf_op jit(solution)/shard_map/ppermute | solution.py:23
  57.1 1.3 %collective-permute-start.23 = (f32[8,128]{1,0:T(8,128)S(1)}, f32[8,128]{1,0:T(8,128)S(1)}, u32[]{:S(2)}, u32[]{:S(2)}) collective-permute-start(f32[8,128]{1,0:T(8,128)S(1)} %chipsum.1.sum_ref), channel_id=1, source_target_pairs={{0,1},{1,0},{2,3},{3,2},{4,5},{5,4},{6,7},{7,6},{8,9},{9,8},{10,11... | collective-permute-start | bytes 12296 | tf_op jit(solution)/shard_map/ppermute | solution.py:23

commit v2 on v1

--- a/solution.py
+++ b/solution.py
@@ -36,25 +36,16 @@
 
 
 VMEM = pl.BlockSpec(memory_space=pltpu.VMEM)
+SMEM = pl.BlockSpec(memory_space=pltpu.SMEM)
 HBM = pl.BlockSpec(memory_space=pltpu.HBM)
 
 
-def split_kernel(dims, cot_hbm, *rest):
+def split_kernel(dims, after_ref, cot_ref, *pair_refs):
     n_seq, head = dims
-    pair_refs, sems = rest[: n_seq // 2], rest[n_seq // 2]
     me = lax.axis_index("seq")
-    loads = []
     for m in range(n_seq):
         at = pl.multiple_of((me ^ m) * head, head)
-        loads.append(
-            pltpu.make_async_copy(
-                cot_hbm.at[:, pl.ds(at, head)], pair_refs[m // 2].at[m % 2], sems.at[m]
-            )
-        )
-    for load in loads:
-        load.start()
-    for load in loads:
-        load.wait()
+        pair_refs[m // 2][m % 2] = cot_ref[:, pl.ds(at, head)]
 
 
 def conv_kernel(dims, frames_hbm, feat_hbm, w_hbm, part_ref, *rest):
@@ -143,26 +134,9 @@
     part_ref[...] = (same + jnp.where(par_at == 1, after, before)).astype(BF16)
 
 
-def table_kernel(dims, after_ref, frames_hbm, group_hbm, offset_hbm, times_hbm, noise_hbm, *rest):
+def table_kernel(dims, frames_ref, group_ref, offset_ref, times_ref, after_ref, raw_ref, *rest):
     fr, cols, clips, n_dp, patch, width = dims
-    pick_ref, scale_ref, noise_ref, live_ref, mark_ref = rest[:5]
-    frames_ref, group_ref, offset_ref, times_ref, raw_ref, sems = rest[5:]
-    loads = [
-        pltpu.make_async_copy(source, target, sems.at[i])
-        for i, (source, target) in enumerate(
-            (
-                (frames_hbm, frames_ref),
-                (group_hbm, group_ref),
-                (offset_hbm, offset_ref),
-                (times_hbm, times_ref),
-                (noise_hbm, raw_ref),
-            )
-        )
-    ]
-    for load in loads:
-        load.start()
-    for load in loads:
-        load.wait()
+    pick_ref, scale_ref, noise_ref, live_ref, mark_ref = rest
     slab = lax.axis_index("dp")
     source = [jnp.int32(-1)] * fr
     owner = [jnp.int32(clips)] * fr
@@ -211,24 +185,14 @@
     send_ref[...] = own.astype(BF16)
 
 
-def weight_kernel(dims, after_ref, embed_hbm, proj_hbm, gains_hbm, out_ref, gains_ref, *rest):
+def weight_kernel(dims, after_ref, embed_ref, proj_ref, out_ref):
     patch, head = dims
-    embed_ref, proj_ref, sems = rest
-    loads = [
-        pltpu.make_async_copy(embed_hbm, embed_ref, sems.at[0]),
-        pltpu.make_async_copy(gains_hbm, gains_ref, sems.at[1]),
-    ] + [pltpu.make_async_copy(proj_hbm.at[i], proj_ref.at[i], sems.at[2 + i]) for i in range(3)]
-    for load in loads:
-        load.start()
-    loads[0].wait()
     for i in range(3):
-        loads[2 + i].wait()
         both = jnp.dot(embed_ref[...], proj_ref[i], preferred_element_type=F32).astype(BF16)
         at = slice(i * head, (i + 1) * head)
         out_ref[:patch, at] = both
         out_ref[patch : 3 * patch, at] = jnp.zeros((2 * patch, head), BF16)
         out_ref[3 * patch :, at] = both
-    loads[1].wait()
 
 
 def mean_of(values):
@@ -243,8 +207,9 @@
     fr, cols, n_seq, patch, head, tile = dims
     tok_refs, cot_refs, rest = rest[:n_seq], rest[n_seq : 2 * n_seq], rest[2 * n_seq :]
     noisy_ref, grad_ref = rest[:2]
-    pairs_refs, rest = rest[2 : 2 + n_seq // 2], rest[2 + n_seq // 2 :]
-    tok_ref, inc_ref, cat_ref, unit_ref, scale_ref, q_ref, k_ref, v_ref, o_ref, dq_ref, dk_ref, dv_ref = rest
+    pair_refs, rest = rest[2 : 2 + n_seq // 2], rest[2 + n_seq // 2 :]
+    tok_ref, inc_ref, cat_ref, unit_ref, scale_ref = rest[:5]
+    q_ref, k_ref, v_ref, o_ref, dq_ref, dk_ref, dv_ref = rest[5:]
     me = lax.axis_index("seq")
     blk = fr * cols
     size = n_seq * blk
@@ -335,64 +300,61 @@
             cat_ref[rows, :], jnp.concatenate(parts, axis=1), TN, preferred_element_type=F32
         )
         grad = term if grad is None else grad + term
-    grad_ref[:patch, :] = (grad[:patch, :] + grad[3 * patch :, :]).astype(BF16)
-    sums = jnp.concatenate(gains + [jnp.zeros((1, head), F32)], axis=1)
+    grad_ref[...] = (grad[:patch, :] + grad[3 * patch :, :]).astype(BF16)
+    sums = jnp.concatenate(gains, axis=0)
     high = sums.astype(BF16).astype(F32)
-    grad_ref[patch:, :] = jnp.concatenate(
-        [high, sums - high, jnp.zeros((EXTRA - 2, 3 * head), F32)], axis=0
-    ).astype(BF16)
+    block = jnp.concatenate([high, sums - high, jnp.zeros((EXTRA - 4, head), F32)], axis=0)
     for m in range(n_seq):
         at = pl.multiple_of((me ^ m) * blk, blk)
-        pairs_refs[m // 2][m % 2] = o_ref[pl.ds(at, blk), :]
+        pair_refs[m // 2][m % 2, :blk] = o_ref[pl.ds(at, blk), :]
+        pair_refs[m // 2][m % 2, blk:] = block.astype(BF16)
 
 
 def proj_kernel(dims, embed_ref, *rest):
-    n_dp, patch, head, rows = dims
+    n_dp, _, head, rows = dims
     grad_refs, (out_ref,) = rest[:n_dp], rest[n_dp:]
     slab = lax.axis_index("dp")
     part = embed_ref[:, pl.ds(pl.multiple_of(slab * rows, rows), rows)]
     left = jnp.concatenate([part] * n_dp, axis=0)
-    right = jnp.concatenate([ref[:patch, :] for ref in grad_refs], axis=0)
+    right = jnp.concatenate([ref[...] for ref in grad_refs], axis=0)
     result = lax.dot_general(left, right, TN, preferred_element_type=F32)
     for i in range(3):
         out_ref[pl.ds(i, rows, stride=3), :] = result[:, i * head : (i + 1) * head]
 
 
+def head_sum_kernel(dims, *rest):
+    n_seq, blk = dims
+    pair_refs, (out_ref, all_ref) = rest[:n_seq], rest[n_seq:]
+    me = lax.axis_index("seq")
+    for m in range(n_seq):
+        pair_ref = pair_refs[m // 2 + (m % 2) * (n_seq // 2)]
+        all_ref[me ^ m] = pair_ref[m % 2, blk:].astype(F32)
+    total = all_ref[0]
+    for h in range(1, n_seq):
+        total = total + all_ref[h]
+    out_ref[...] = total[:8] + pltpu.roll(total, EXTRA - 2, 0)[:8]
+
+
 def group_sum_kernel(dims, *rest):
-    n_dp, patch, head = dims
-    grad_refs, (out_ref, all_ref) = rest[:n_dp], rest[n_dp:]
+    (n_dp,) = dims
+    sum_refs, (out_ref, all_ref) = rest[:n_dp], rest[n_dp:]
     slab = lax.axis_index("dp")
     for m in range(n_dp):
-        all_ref[slab ^ m] = grad_refs[m][patch:, :].astype(F32)
+        all_ref[slab ^ m] = sum_refs[m][...]
     total = all_ref[0]
     for g in range(1, n_dp):
         total = total + all_ref[g]
-    both = total[0:1, :] + total[1:2, :]
-    out_ref[...] = jnp.concatenate(
-        [both[:, :head], both[:, head : 2 * head], jnp.zeros((6, head), F32)], axis=0
-    )
-
-
-def chip_sum_kernel(dims, *rest):
-    (half,) = dims
-    sum_refs, (out_ref, all_ref) = rest[:half], rest[half:]
-    chip = lax.axis_index("seq") // 2
-    for m in range(half):
-        all_ref[chip ^ m] = sum_refs[m][...]
-    total = all_ref[0]
-    for z in range(1, half):
-        total = total + all_ref[z]
-    out_ref[...] = total
-
-
-def finish_kernel(dims, sum_ref, other_ref, *rest):
-    n_seq, head = dims
-    pair_refs, (out_ref, gain_ref) = rest[:n_seq], rest[n_seq:]
+    out_ref[...] = total[:2]
+
+
+def finish_kernel(dims, *rest):
+    n_seq, blk, head = dims
+    pair_refs, (out_ref,) = rest[:n_seq], rest[n_seq:]
     me = lax.axis_index("seq")
     for m in range(n_seq):
         at = pl.multiple_of((me ^ m) * head, head)
-        out_ref[:, pl.ds(at, head)] = pair_refs[m // 2 + (m % 2) * (n_seq // 2)][m % 2]
-    gain_ref[...] = sum_ref[0:2, :] + other_ref[0:2, :]
+        pair_ref = pair_refs[m // 2 + (m % 2) * (n_seq // 2)]
+        out_ref[:, pl.ds(at, head)] = pair_ref[m % 2, :blk]
 
 
 def body(
@@ -423,20 +385,6 @@
     rows_out = (fr + 2) * cols
     tile = min(512, size)
 
-    half = n_seq // 2
-    cots = pl.pallas_call(
-        functools.partial(split_kernel, (n_seq, head)),
-        out_shape=[S((2, blk, head), BF16)] * half,
-        in_specs=[HBM],
-        out_specs=[VMEM] * half,
-        scratch_shapes=[pltpu.SemaphoreType.DMA((n_seq,))],
-        compiler_params=params(),
-        cost_estimate=cost(0, 4 * blk * n_seq * head),
-        name="split",
-    )(*keep_in(pltpu.HBM, cotangent.reshape(blk, n_seq * head)))
-    cots = [cots[0]] + [swap(cots[m], "seq", 2 * m) for m in range(1, half)]
-    cots += [swap(pair, "seq", 1) for pair in cots]
-
     partial = pl.pallas_call(
         functools.partial(conv_kernel, (fr, wd, ch, lat, clips)),
         out_shape=S((rows_out, lanes), BF16),
@@ -462,21 +410,27 @@
         )
     )
     parts = [partial] + [swap(partial, "dp", m) for m in range(1, n_dp)]
+    half = n_seq // 2
+    cots = pl.pallas_call(
+        functools.partial(split_kernel, (n_seq, head)),
+        out_shape=[S((2, blk, head), BF16)] * half,
+        in_specs=[VMEM] * 2,
+        out_specs=[VMEM] * half,
+        compiler_params=params(),
+        cost_estimate=cost(0, 4 * blk * n_seq * head),
+        name="split",
+    )(partial, cotangent.reshape(blk, n_seq * head))
+    cots = [cots[0]] + [swap(cots[m], "seq", 2 * m) for m in range(1, half)]
+    cots += [swap(pair, "seq", 1) for pair in cots]
     pick, scale, noise, live, mark = pl.pallas_call(
         functools.partial(table_kernel, (fr, cols, clips, n_dp, patch, lanes)),
         out_shape=[S((blk, n_dp * rows_out), BF16)] + [S((blk, lanes), F32)] * 4,
-        in_specs=[VMEM] + [HBM] * 5,
+        in_specs=[SMEM] * 4 + [VMEM] * 2,
         out_specs=[VMEM] * 5,
-        scratch_shapes=[pltpu.SMEM((clips,), jnp.int32)] * 3
-        + [
-            pltpu.SMEM((clips,), F32),
-            pltpu.VMEM((patch, blk), BF16),
-            pltpu.SemaphoreType.DMA((5,)),
-        ],
         compiler_params=params(),
         cost_estimate=cost(2**22, 2**21),
         name="tables",
-    )(partial, clip_frames, clip_group, clip_offset, clip_times, noise_tokens[0].T)
+    )(clip_frames, clip_group, clip_offset, clip_times, partial, noise_tokens[0].T)
 
     send, own = pl.pallas_call(
         functools.partial(slot_kernel, (n_dp,)),
@@ -492,26 +446,21 @@
         toks[m] = swap(send, "seq", m)
     for m in range(0, n_seq, 2):
         toks[m + 1] = swap(toks[m], "seq", 1)
-    weights, gains = pl.pallas_call(
+    weights = pl.pallas_call(
         functools.partial(weight_kernel, (patch, head)),
-        out_shape=[S((4 * patch, 3 * head), BF16), S((2, head), F32)],
-        in_specs=[VMEM] + [HBM] * 3,
-        out_specs=[VMEM] * 2,
-        scratch_shapes=[
-            pltpu.VMEM((patch, model), BF16),
-            pltpu.VMEM((3, model, head), BF16),
-            pltpu.SemaphoreType.DMA((5,)),
-        ],
+        out_shape=S((4 * patch, 3 * head), BF16),
+        in_specs=[VMEM] * 3,
+        out_specs=VMEM,
         compiler_params=params(),
         cost_estimate=cost(2 * patch * model * 3 * head, 2 * model * (3 * head + patch)),
         name="weights",
-    )(send, embed_weight, attention_proj.transpose(1, 2, 0, 3).reshape(3, model, head), norm_gains)
+    )(send, embed_weight, attention_proj.transpose(1, 2, 0, 3).reshape(3, model, head))
 
     wide = 2 * head
     noisy, grad, *pairs = pl.pallas_call(
         functools.partial(attention_kernel, (fr, cols, n_seq, patch, head, tile)),
-        out_shape=[S((patch, blk), F32), S((patch + EXTRA, 3 * head), BF16)]
-        + [S((2, blk, head), BF16)] * half,
+        out_shape=[S((patch, blk), F32), S((patch, 3 * head), BF16)]
+        + [S((2, blk + EXTRA, head), BF16)] * half,
         in_specs=[VMEM] * (5 + 2 * n_seq),
         out_specs=[VMEM] * (2 + half),
         scratch_shapes=[
@@ -531,33 +480,32 @@
         compiler_params=params(),
         cost_estimate=cost(12 * size * size * head, 2**21, size * size),
         name="attention",
-    )(gains, weights, own, live, mark, *toks, *cots)
+    )(norm_gains, weights, own, live, mark, *toks, *cots)
 
     pairs = [pairs[0]] + [swap(pairs[m], "seq", 2 * m) for m in range(1, half)]
     grads = [grad] + [swap(grad, "dp", m) for m in range(1, n_dp)]
+    pairs += [swap(pair, "seq", 1) for pair in pairs]
     gain = pl.pallas_call(
-        functools.partial(group_sum_kernel, (n_dp, patch, head)),
+        functools.partial(head_sum_kernel, (n_seq, blk)),
         out_shape=S((8, head), F32),
+        in_specs=[VMEM] * n_seq,
+        out_specs=VMEM,
+        scratch_shapes=[pltpu.VMEM((n_seq, EXTRA, head), F32)],
+        compiler_params=params(),
+        cost_estimate=cost(0, 2**12),
+        name="headsum",
+    )(*pairs)
+    gain = [gain] + [swap(gain, "dp", m) for m in range(1, n_dp)]
+    norm_grad = pl.pallas_call(
+        functools.partial(group_sum_kernel, (n_dp,)),
+        out_shape=S((2, head), F32),
         in_specs=[VMEM] * n_dp,
         out_specs=VMEM,
-        scratch_shapes=[pltpu.VMEM((n_dp, EXTRA, 3 * head), F32)],
+        scratch_shapes=[pltpu.VMEM((n_dp, 8, head), F32)],
         compiler_params=params(),
         cost_estimate=cost(0, 2**12),
         name="groupsum",
-    )(*grads)
-    gain = [gain] + [swap(gain, "seq", 2 * m) for m in range(1, half)]
-    gain = pl.pallas_call(
-        functools.partial(chip_sum_kernel, (half,)),
-        out_shape=S((8, head), F32),
-        in_specs=[VMEM] * half,
-        out_specs=VMEM,
-        scratch_shapes=[pltpu.VMEM((half, 8, head), F32)],
-        compiler_params=params(),
-        cost_estimate=cost(0, 2**12),
-        name="chipsum",
     )(*gain)
-    other = swap(gain, "seq", 1)
-    pairs += [swap(pair, "seq", 1) for pair in pairs]
     rows = model // n_dp
     proj_grad = pl.pallas_call(
         functools.partial(proj_kernel, (n_dp, patch, head, rows)),
@@ -568,15 +516,15 @@
         cost_estimate=cost(2 * rows * 3 * head * patch * n_dp, 4 * rows * 3 * head),
         name="projgrad",
     )(embed_weight, *grads)
-    out, norm_grad = pl.pallas_call(
-        functools.partial(finish_kernel, (n_seq, head)),
-        out_shape=[S((blk, n_seq * head), BF16), S((2, head), F32)],
-        in_specs=[VMEM] * (2 + n_seq),
-        out_specs=[VMEM] * 2,
+    out = pl.pallas_call(
+        functools.partial(finish_kernel, (n_seq, blk, head)),
+        out_shape=S((blk, n_seq * head), BF16),
+        in_specs=[VMEM] * n_seq,
+        out_specs=VMEM,
         compiler_params=params(),
         cost_estimate=cost(0, 4 * blk * n_seq * head),
         name="finish",
-    )(gain, other, *pairs)
+    )(*pairs)
     return (
         noisy.T[None],
         out[None],

time: 59.4 us -> 51.7 us (0.87)
  waiting for transfers between devices: 18.4 us -> 9.66 us
  starting transfers between devices: 26.4 us -> 28.3 us
  Pallas kernels: 13.5 us -> 12.7 us
    ppermute x31 -> x30, waiting for transfers between devices: 18.4 us -> 9.66 us  [swap(): lax.ppermute(block, axis, [(i, i ^ mask) for i in range(lax.axis_size(axi...]
    ppermute x31 -> x30, starting transfers between devices: 26.4 us -> 28.3 us  [swap(): lax.ppermute(block, axis, [(i, i ^ mask) for i in range(lax.axis_size(axi...]
    pallas_call x1, Pallas kernels: 0.94 us -> 0.07 us  [body(): pl.pallas_call(functools.partial(split_kernel, (n_seq, head)), out_shape=...]
  transfers between devices with their start and end apart: 31 -> 30, of which waited for: 7 -> 8; matrix products, arithmetic and copies ran while one was open for 0% -> 0% of each run, Pallas kernels for 7% -> 7%
where the time goes in v2:
time: 51.7 us; the launch traced here: 51.6 us
  starting transfers between devices  28.3 us (55%)
  Pallas kernels  12.7 us (25%)
  waiting for transfers between devices  9.66 us (19%)
  between operations  0.83 us (2%)
    ppermute x30, starting transfers between devices, swap(): lax.ppermute(block, axis, [(i, i ^ mask) for i in range(lax.axis_size(axi...  28.3 us
    ppermute x30, waiting for transfers between devices, swap(): lax.ppermute(block, axis, [(i, i ^ mask) for i in range(lax.axis_size(axi...  9.66 us
    pallas_call x1, Pallas kernels, body(): pl.pallas_call(functools.partial(attention_kernel, (fr, cols, n_seq, patc...  5.68 us
    pallas_call x1, Pallas kernels, body(): pl.pallas_call(functools.partial(conv_kernel, (fr, wd, ch, lat, clips)),...  2.77 us
    pallas_call x1, Pallas kernels, body(): pl.pallas_call(functools.partial(proj_kernel, (n_dp, patch, head, rows)),...  1.21 us
    pallas_call x1, Pallas kernels, body(): pl.pallas_call(functools.partial(table_kernel, (fr, cols, clips, n_dp, pa...  1.05 us
  transfers between devices with their start and end apart: 30, of which 8 were waited for; matrix products, arithmetic and copies ran while one was open for 0% of the time, Pallas kernels for 7%

profile of v2, /device:TPU:0, one launch (start us, length us, event | category | flops | bytes accessed | tf_op | source)
XLA Modules:
  0.0 51.6 jit_solution(11018798811289388468)
XLA Ops:
  0.7 2.8 %conv.1.after_ref.rest_0_ = bf16[160,128]{1,0:T(8,128)(2,1)S(1)} custom-call(s32[8]{0:T(128)} %frames_ref.1, bf16[512,512]{1,0:T(8,128)(2,1)} %bitcast.21, bf16[432,512]{1,0:T(8,128)(2,1)} %bitcast.22), custom_call_target="tpu_custom_call" | custom-call | flops 402653184 | bytes 2097152 | tf_op jit(solution)/shard_map/conv/pallas_call | solution.py:388
  3.5 0.0 copy-start.8
  3.5 4.0 %collective-permute-start.2 = (bf16[160,128]{1,0:T(8,128)(2,1)S(1)}, bf16[160,128]{1,0:T(8,128)(2,1)S(1)}, u32[]{:S(2)}, u32[]{:S(2)}) collective-permute-start(bf16[160,128]{1,0:T(8,128)(2,1)S(1)} %conv.1.after_ref.rest_0_), channel_id=1, source_target_pairs={{0,24},{8,16},{16,8},{24,0},{1,25},{9,17},{17,9},{25,1},{2,26},{10... | collective-permute-start | bytes 122888 | tf_op jit(solution)/shard_map/ppermute | solution.py:23
  7.5 0.5 collective-permute-start.1
  8.0 0.1 split.1
  8.1 1.6 %collective-permute-start.10 = (bf16[2,128,128]{2,1,0:T(8,128)(2,1)S(1)}, bf16[2,128,128]{2,1,0:T(8,128)(2,1)S(1)}, u32[]{:S(2)}, u32[]{:S(2)}) collective-permute-start(bf16[2,128,128]{2,1,0:T(8,128)(2,1)S(1)} %get-tuple-element.29), channel_id=1, source_target_pairs={{0,2},{1,3},{2,0},{3,1},{4,6},{5,7},{6,4},{7,5},{8,10},{9,11},{10,... | collective-permute-start | bytes 196616 | tf_op jit(solution)/shard_map/ppermute | solution.py:23
  9.7 2.6 %collective-permute-start.11 = (bf16[2,128,128]{2,1,0:T(8,128)(2,1)S(1)}, bf16[2,128,128]{2,1,0:T(8,128)(2,1)S(1)}, u32[]{:S(2)}, u32[]{:S(2)}) collective-permute-start(bf16[2,128,128]{2,1,0:T(8,128)(2,1)S(1)} %get-tuple-element.30), channel_id=1, source_target_pairs={{0,4},{1,5},{2,6},{3,7},{4,0},{5,1},{6,2},{7,3},{8,12},{9,13},{10,... | collective-permute-start | bytes 196616 | tf_op jit(solution)/shard_map/ppermute | solution.py:23
  12.3 0.5 %collective-permute-start = (bf16[160,128]{1,0:T(8,128)(2,1)S(1)}, bf16[160,128]{1,0:T(8,128)(2,1)S(1)}, u32[]{:S(2)}, u32[]{:S(2)}) collective-permute-start(bf16[160,128]{1,0:T(8,128)(2,1)S(1)} %conv.1.after_ref.rest_0_), channel_id=1, source_target_pairs={{0,8},{8,0},{16,24},{24,16},{1,9},{9,1},{17,25},{25,17},{2,10},{10... | collective-permute-start | bytes 122888 | tf_op jit(solution)/shard_map/ppermute | solution.py:23
  12.8 0.0 collective-permute-done.2.rest_3_
  12.8 0.7 %collective-permute-start.12 = (bf16[2,128,128]{2,1,0:T(8,128)(2,1)S(1)}, bf16[2,128,128]{2,1,0:T(8,128)(2,1)S(1)}, u32[]{:S(2)}, u32[]{:S(2)}) collective-permute-start(bf16[2,128,128]{2,1,0:T(8,128)(2,1)S(1)} %get-tuple-element.31), channel_id=1, source_target_pairs={{0,6},{1,7},{2,4},{3,5},{4,2},{5,3},{6,0},{7,1},{8,14},{9,15},{10,... | collective-permute-start | bytes 196616 | tf_op jit(solution)/shard_map/ppermute | solution.py:23
  13.6 0.0 collective-permute-done.1.rest_2_
  13.6 0.0 collective-permute-start.13
  13.6 1.0 %tables.1 = (bf16[128,640]{1,0:T(8,128)(2,1)S(1)}, f32[128,128]{1,0:T(8,128)S(1)}, f32[128,128]{1,0:T(8,128)S(1)}, f32[128,128]{1,0:T(8,128)S(1)}, f32[128,128]{1,0:T(8,128)S(1)}) custom-call(s32[8]{0:T(128)S(1)} %copy-done.4, s32[8]{0:T(128)S(1)} %copy-done.5, s32[8]{0:T(128)S(1)} %copy-done.6, f32[8]{0:T(128)S(1)} %copy-done.7, ...), custom_call_target="tpu_custom_call" | custom-call | flops 4194304 | bytes 2097152 | tf_op jit(solution)/shard_map/tables/pallas_call | solution.py:425
  14.7 1.6 %collective-permute-done.rest_1_ = bf16[160,128]{1,0:T(8,128)(2,1)S(1)} collective-permute-done((bf16[160,128]{1,0:T(8,128)(2,1)S(1)}, bf16[160,128]{1,0:T(8,128)(2,1)S(1)}, u32[]{:S(2)}, u32[]{:S(2)}) %collective-permute-start) | collective-permute-done | bytes 40992 | tf_op jit(solution)/shard_map/ppermute | solution.py:23
  16.3 0.2 slots.1
  16.5 1.5 %collective-permute-start.8 = (bf16[128,128]{1,0:T(8,128)(2,1)S(1)}, bf16[128,128]{1,0:T(8,128)(2,1)S(1)}, u32[]{:S(2)}, u32[]{:S(2)}) collective-permute-start(bf16[128,128]{1,0:T(8,128)(2,1)S(1)} %get-tuple-element.24.after_ref.rest_0_), channel_id=1, source_target_pairs={{0,6},{1,7},{2,4},{3,5},{4,2},{5,3},{6,0},{7,1},{8,14},{9,15},{10,... | collective-permute-start | bytes 98312 | tf_op jit(solution)/shard_map/ppermute | solution.py:23
  18.0 0.0 collective-permute-done.10.rest_9_
  18.0 0.4 collective-permute-start.6
  18.5 2.5 %collective-permute-start.4 = (bf16[128,128]{1,0:T(8,128)(2,1)S(1)}, bf16[128,128]{1,0:T(8,128)(2,1)S(1)}, u32[]{:S(2)}, u32[]{:S(2)}) collective-permute-start(bf16[128,128]{1,0:T(8,128)(2,1)S(1)} %get-tuple-element.24.after_ref.rest_0_), channel_id=1, source_target_pairs={{0,2},{1,3},{2,0},{3,1},{4,6},{5,7},{6,4},{7,5},{8,10},{9,11},{10,... | collective-permute-start | bytes 98312 | tf_op jit(solution)/shard_map/ppermute | solution.py:23
  21.0 0.5 collective-permute-start.14
  21.5 0.9 %collective-permute-done.8.rest_6_ = bf16[128,128]{1,0:T(8,128)(2,1)S(1)} collective-permute-done((bf16[128,128]{1,0:T(8,128)(2,1)S(1)}, bf16[128,128]{1,0:T(8,128)(2,1)S(1)}, u32[]{:S(2)}, u32[]{:S(2)}) %collective-permute-start.8) | collective-permute-done | bytes 32800 | tf_op jit(solution)/shard_map/ppermute | solution.py:23
  22.4 0.9 %collective-permute-done.6.rest_4_ = bf16[128,128]{1,0:T(8,128)(2,1)S(1)} collective-permute-done((bf16[128,128]{1,0:T(8,128)(2,1)S(1)}, bf16[128,128]{1,0:T(8,128)(2,1)S(1)}, u32[]{:S(2)}, u32[]{:S(2)}) %collective-permute-start.6) | collective-permute-done | bytes 32800 | tf_op jit(solution)/shard_map/ppermute | solution.py:23
  23.3 0.0 collective-permute-start.15
  23.3 0.0 collective-permute-done.4.rest_2_
  23.3 0.5 collective-permute-start.16
  23.8 0.1 collective-permute-start.7
  23.8 0.4 collective-permute-start.5
  24.3 0.4 weights.1.w_ref
  24.7 0.3 collective-permute-done.7.rest_5_
  25.0 0.2 collective-permute-done.5.rest_3_
  25.2 5.7 %attention.1 = (f32[64,128]{1,0:T(8,128)}, bf16[64,384]{1,0:T(8,128)(2,1)S(1)}, bf16[2,144,128]{2,1,0:T(8,128)(2,1)S(1)}, bf16[2,144,128]{2,1,0:T(8,128)(2,1)S(1...) custom-call(f32[2,128]{1,0:T(2,128)S(1)} %copy-done.8, bf16[256,384]{1,0:T(8,128)(2,1)S(1)} %weights.1.w_ref, ...), custom_call_target="tpu_custom_call" | custom-call | flops 1610612736 | bytes 2097152 | tf_op jit(solution)/shard_map/attention/pallas_call | solution.py:460
  30.9 1.5 %collective-permute-start.17 = (bf16[2,144,128]{2,1,0:T(8,128)(2,1)S(1)}, bf16[2,144,128]{2,1,0:T(8,128)(2,1)S(1)}, u32[]{:S(2)}, u32[]{:S(2)}) collective-permute-start(bf16[2,144,128]{2,1,0:T(8,128)(2,1)S(1)} %get-tuple-element.34), channel_id=1, source_target_pairs={{0,2},{1,3},{2,0},{3,1},{4,6},{5,7},{6,4},{7,5},{8,10},{9,11},{10,... | collective-permute-start | bytes 221192 | tf_op jit(solution)/shard_map/ppermute | solution.py:23
  32.3 1.1 %collective-permute-start.18 = (bf16[2,144,128]{2,1,0:T(8,128)(2,1)S(1)}, bf16[2,144,128]{2,1,0:T(8,128)(2,1)S(1)}, u32[]{:S(2)}, u32[]{:S(2)}) collective-permute-start(bf16[2,144,128]{2,1,0:T(8,128)(2,1)S(1)} %get-tuple-element.35), channel_id=1, source_target_pairs={{0,4},{1,5},{2,6},{3,7},{4,0},{5,1},{6,2},{7,3},{8,12},{9,13},{10,... | collective-permute-start | bytes 221192 | tf_op jit(solution)/shard_map/ppermute | solution.py:23
  33.4 1.9 %collective-permute-start.19 = (bf16[2,144,128]{2,1,0:T(8,128)(2,1)S(1)}, bf16[2,144,128]{2,1,0:T(8,128)(2,1)S(1)}, u32[]{:S(2)}, u32[]{:S(2)}) collective-permute-start(bf16[2,144,128]{2,1,0:T(8,128)(2,1)S(1)} %get-tuple-element.36), channel_id=1, source_target_pairs={{0,6},{1,7},{2,4},{3,5},{4,2},{5,3},{6,0},{7,1},{8,14},{9,15},{10,... | collective-permute-start | bytes 221192 | tf_op jit(solution)/shard_map/ppermute | solution.py:23
  35.2 0.1 collective-permute-done.17.rest_1_
  35.4 0.4 collective-permute-start.21
  35.8 5.2 %collective-permute-done.18.rest_2_ = bf16[2,144,128]{2,1,0:T(8,128)(2,1)S(1)} collective-permute-done((bf16[2,144,128]{2,1,0:T(8,128)(2,1)S(1)}, bf16[2,144,128]{2,1,0:T(8,128)(2,1)S(1)}, u32[]{:S(2)}, u32[]{:S(2)}) %collective-permute-start.18) | collective-permute-done | bytes 73760 | tf_op jit(solution)/shard_map/ppermute | solution.py:23
  41.0 0.5 collective-permute-start.23
  41.5 1.8 %collective-permute-start.26 = (bf16[64,384]{1,0:T(8,128)(2,1)S(1)}, bf16[64,384]{1,0:T(8,128)(2,1)S(1)}, u32[]{:S(2)}, u32[]{:S(2)}) collective-permute-start(bf16[64,384]{1,0:T(8,128)(2,1)S(1)} %get-tuple-element.37.rest_0_), channel_id=1, source_target_pairs={{0,24},{8,16},{16,8},{24,0},{1,25},{9,17},{17,9},{25,1},{2,26},{10... | collective-permute-start | bytes 147464 | tf_op jit(solution)/shard_map/ppermute | solution.py:23
  43.3 0.5 collective-permute-start.25
  43.8 1.2 %collective-permute-start.24 = (bf16[64,384]{1,0:T(8,128)(2,1)S(1)}, bf16[64,384]{1,0:T(8,128)(2,1)S(1)}, u32[]{:S(2)}, u32[]{:S(2)}) collective-permute-start(bf16[64,384]{1,0:T(8,128)(2,1)S(1)} %get-tuple-element.37.rest_0_), channel_id=1, source_target_pairs={{0,8},{8,0},{16,24},{24,16},{1,9},{9,1},{17,25},{25,17},{2,10},{10... | collective-permute-start | bytes 147464 | tf_op jit(solution)/shard_map/ppermute | solution.py:23
  45.0 1.9 %collective-permute-start.29 = (f32[8,128]{1,0:T(8,128)S(1)}, f32[8,128]{1,0:T(8,128)S(1)}, u32[]{:S(2)}, u32[]{:S(2)}) collective-permute-start(f32[8,128]{1,0:T(8,128)S(1)} %headsum.1.rest_0_), channel_id=1, source_target_pairs={{0,24},{8,16},{16,8},{24,0},{1,25},{9,17},{17,9},{25,1},{2,26},{10... | collective-permute-start | bytes 12296 | tf_op jit(solution)/shard_map/ppermute | solution.py:23
  46.9 0.5 collective-permute-start.28
  47.4 1.2 %collective-permute-start.27 = (f32[8,128]{1,0:T(8,128)S(1)}, f32[8,128]{1,0:T(8,128)S(1)}, u32[]{:S(2)}, u32[]{:S(2)}) collective-permute-start(f32[8,128]{1,0:T(8,128)S(1)} %headsum.1.rest_0_), channel_id=1, source_target_pairs={{0,8},{8,0},{16,24},{24,16},{1,9},{9,1},{17,25},{25,17},{2,10},{10... | collective-permute-start | bytes 12296 | tf_op jit(solution)/shard_map/ppermute | solution.py:23
  48.6 1.2 %projgrad.1 = f32[1536,128]{1,0:T(8,128)} custom-call(bf16[64,2048]{1,0:T(8,128)(2,1)S(1)} %copy-done.1, bf16[64,384]{1,0:T(8,128)(2,1)S(1)} %get-tuple-element.37.rest_0_, bf16[64,384]{1,0:T(8,128)(2,1)S(1)} %collective-permute-done.24.rest_1_, bf16[64,384]{1,0:T(8,128)(2,1)S(1)} %collective-permute-done.25.rest_2_, ...), custom_call_target="tpu_custom_call" | custom-call | flops 100663296 | bytes 786432 | tf_op jit(solution)/shard_map/projgrad/pallas_call | solution.py:510
  49.8 0.8 %finish.1 = bf16[128,1024]{1,0:T(8,128)(2,1)} custom-call(bf16[2,144,128]{2,1,0:T(8,128)(2,1)S(1)} %get-tuple-element.33.rest_0_, bf16[2,144,128]{2,1,0:T(8,128)(2,1)S(1)} %collective-permute-done.17.rest_1_, bf16[2,144,128]{2,1,0:T(8,128)(2,1)S(1)} %collective-permute-done.18.rest_2_, bf16[2,144,128]{2,1,0:T(8,128)(2,1)S(1)} %collective-permute-done.19.rest_3_, ...), custom_call_target="tpu_custom_call" | custom-call | bytes 524288 | tf_op jit(solution)/shard_map/finish/pallas_call | solution.py:519
  50.5 0.4 collective-permute-done.27.rest_1_
  51.0 0.6 %groupsum.1 = f32[2,128]{1,0:T(2,128)} custom-call(f32[8,128]{1,0:T(8,128)S(1)} %headsum.1.rest_0_, f32[8,128]{1,0:T(8,128)S(1)} %collective-permute-done.27.rest_1_, f32[8,128]{1,0:T(8,128)S(1)} %collective-permute-done.28.rest_2_, f32[8,128]{1,0:T(8,128)S(1)} %collective-permute-done.29.rest_3_), custom_call_target="tpu_custom_call" | custom-call | bytes 4096 | tf_op jit(solution)/shard_map/groupsum/pallas_call | solution.py:499
  (40 shorter events, 0.1 us)
Async XLA Ops:
  0.6 12.9 %copy-start.4 = (s32[8]{0:T(128)S(1)}, s32[8]{0:T(128)}, u32[]{:S(2)}) copy-start(s32[8]{0:T(128)} %frames_ref.1) | copy-start | bytes 100
  0.6 7.4 %copy-start.2 = (bf16[1,128,1024]{2,1,0:T(8,128)(2,1)S(1)}, bf16[1,128,1024]{2,1,0:T(8,128)(2,1)}, u32[]{:S(2)}) copy-start(bf16[1,128,1024]{2,1,0:T(8,128)(2,1)} %param.21) | copy-start | bytes 786436
  0.7 12.9 %copy-start.3 = (bf16[1,128,64]{1,2,0:T(8,128)(2,1)S(1)}, bf16[1,128,64]{1,2,0:T(8,128)(2,1)}, u32[]{:S(2)}) copy-start(bf16[1,128,64]{1,2,0:T(8,128)(2,1)} %param.17) | copy-start | bytes 49156
  0.7 12.9 %copy-start.7 = (f32[8]{0:T(128)S(1)}, f32[8]{0:T(128)}, u32[]{:S(2)}) copy-start(f32[8]{0:T(128)} %times_ref.1) | copy-start | bytes 100
  0.7 12.9 %copy-start.6 = (s32[8]{0:T(128)S(1)}, s32[8]{0:T(128)}, u32[]{:S(2)}) copy-start(s32[8]{0:T(128)} %offset_ref.1) | copy-start | bytes 100
  0.7 12.9 %copy-start.5 = (s32[8]{0:T(128)S(1)}, s32[8]{0:T(128)}, u32[]{:S(2)}) copy-start(s32[8]{0:T(128)} %group_ref.1) | copy-start | bytes 100
  0.7 23.6 %copy-start.1 = (bf16[64,2048]{1,0:T(8,128)(2,1)S(1)}, bf16[64,2048]{1,0:T(8,128)(2,1)}, u32[]{:S(2)}) copy-start(bf16[64,2048]{1,0:T(8,128)(2,1)} %embed_ref.3) | copy-start | bytes 786436
  0.7 23.6 %copy-start = (bf16[2048,3,1,128]{3,0,2,1:T(8,128)(2,1)S(1)}, bf16[2048,3,1,128]{3,0,2,1:T(8,128)(2,1)}, u32[]{:S(2)}) copy-start(bf16[2048,3,1,128]{3,0,2,1:T(8,128)(2,1)} %param.19) | copy-start | bytes 4718596
  3.5 21.7 %copy-start.8 = (f32[2,128]{1,0:T(2,128)S(1)}, f32[2,128]{1,0:T(2,128)}, u32[]{:S(2)}) copy-start(f32[2,128]{1,0:T(2,128)} %gains_ref.1) | copy-start | bytes 3076
  3.5 9.3 %collective-permute-start.2 = (bf16[160,128]{1,0:T(8,128)(2,1)S(1)}, bf16[160,128]{1,0:T(8,128)(2,1)S(1)}, u32[]{:S(2)}, u32[]{:S(2)}) collective-permute-start(bf16[160,128]{1,0:T(8,128)(2,1)S(1)} %conv.1.after_ref.rest_0_), channel_id=1, source_target_pairs={{0,24},{8,16},{16,8},{24,0},{1,25},{9,17},{17,9},{25,1},{2,26},{10... | collective-permute-start | bytes 122888 | tf_op jit(solution)/shard_map/ppermute | solution.py:23
  7.5 6.1 %collective-permute-start.1 = (bf16[160,128]{1,0:T(8,128)(2,1)S(1)}, bf16[160,128]{1,0:T(8,128)(2,1)S(1)}, u32[]{:S(2)}, u32[]{:S(2)}) collective-permute-start(bf16[160,128]{1,0:T(8,128)(2,1)S(1)} %conv.1.after_ref.rest_0_), channel_id=1, source_target_pairs={{0,16},{8,24},{16,0},{24,8},{1,17},{9,25},{17,1},{25,9},{2,18},{10... | collective-permute-start | bytes 122888 | tf_op jit(solution)/shard_map/ppermute | solution.py:23
  8.1 10.0 %collective-permute-start.10 = (bf16[2,128,128]{2,1,0:T(8,128)(2,1)S(1)}, bf16[2,128,128]{2,1,0:T(8,128)(2,1)S(1)}, u32[]{:S(2)}, u32[]{:S(2)}) collective-permute-start(bf16[2,128,128]{2,1,0:T(8,128)(2,1)S(1)} %get-tuple-element.29), channel_id=1, source_target_pairs={{0,2},{1,3},{2,0},{3,1},{4,6},{5,7},{6,4},{7,5},{8,10},{9,11},{10,... | collective-permute-start | bytes 196616 | tf_op jit(solution)/shard_map/ppermute | solution.py:23
  9.7 8.8 %collective-permute-start.11 = (bf16[2,128,128]{2,1,0:T(8,128)(2,1)S(1)}, bf16[2,128,128]{2,1,0:T(8,128)(2,1)S(1)}, u32[]{:S(2)}, u32[]{:S(2)}) collective-permute-start(bf16[2,128,128]{2,1,0:T(8,128)(2,1)S(1)} %get-tuple-element.30), channel_id=1, source_target_pairs={{0,4},{1,5},{2,6},{3,7},{4,0},{5,1},{6,2},{7,3},{8,12},{9,13},{10,... | collective-permute-start | bytes 196616 | tf_op jit(solution)/shard_map/ppermute | solution.py:23
  12.3 4.0 %collective-permute-start = (bf16[160,128]{1,0:T(8,128)(2,1)S(1)}, bf16[160,128]{1,0:T(8,128)(2,1)S(1)}, u32[]{:S(2)}, u32[]{:S(2)}) collective-permute-start(bf16[160,128]{1,0:T(8,128)(2,1)S(1)} %conv.1.after_ref.rest_0_), channel_id=1, source_target_pairs={{0,8},{8,0},{16,24},{24,16},{1,9},{9,1},{17,25},{25,17},{2,10},{10... | collective-permute-start | bytes 122888 | tf_op jit(solution)/shard_map/ppermute | solution.py:23
  12.8 8.1 %collective-permute-start.12 = (bf16[2,128,128]{2,1,0:T(8,128)(2,1)S(1)}, bf16[2,128,128]{2,1,0:T(8,128)(2,1)S(1)}, u32[]{:S(2)}, u32[]{:S(2)}) collective-permute-start(bf16[2,128,128]{2,1,0:T(8,128)(2,1)S(1)} %get-tuple-element.31), channel_id=1, source_target_pairs={{0,6},{1,7},{2,4},{3,5},{4,2},{5,3},{6,0},{7,1},{8,14},{9,15},{10,... | collective-permute-start | bytes 196616 | tf_op jit(solution)/shard_map/ppermute | solution.py:23
  13.6 7.4 %collective-permute-start.13 = (bf16[2,128,128]{2,1,0:T(8,128)(2,1)S(1)}, bf16[2,128,128]{2,1,0:T(8,128)(2,1)S(1)}, u32[]{:S(2)}, u32[]{:S(2)}) collective-permute-start(bf16[2,128,128]{2,1,0:T(8,128)(2,1)S(1)} %get-tuple-element.28.rest_8_), channel_id=1, source_target_pairs={{0,1},{1,0},{2,3},{3,2},{4,5},{5,4},{6,7},{7,6},{8,9},{9,8},{10,11... | collective-permute-start | bytes 196616 | tf_op jit(solution)/shard_map/ppermute | solution.py:23
  16.5 5.9 %collective-permute-start.8 = (bf16[128,128]{1,0:T(8,128)(2,1)S(1)}, bf16[128,128]{1,0:T(8,128)(2,1)S(1)}, u32[]{:S(2)}, u32[]{:S(2)}) collective-permute-start(bf16[128,128]{1,0:T(8,128)(2,1)S(1)} %get-tuple-element.24.after_ref.rest_0_), channel_id=1, source_target_pairs={{0,6},{1,7},{2,4},{3,5},{4,2},{5,3},{6,0},{7,1},{8,14},{9,15},{10,... | collective-permute-start | bytes 98312 | tf_op jit(solution)/shard_map/ppermute | solution.py:23
  18.0 5.2 %collective-permute-start.6 = (bf16[128,128]{1,0:T(8,128)(2,1)S(1)}, bf16[128,128]{1,0:T(8,128)(2,1)S(1)}, u32[]{:S(2)}, u32[]{:S(2)}) collective-permute-start(bf16[128,128]{1,0:T(8,128)(2,1)S(1)} %get-tuple-element.24.after_ref.rest_0_), channel_id=1, source_target_pairs={{0,4},{1,5},{2,6},{3,7},{4,0},{5,1},{6,2},{7,3},{8,12},{9,13},{10,... | collective-permute-start | bytes 98312 | tf_op jit(solution)/shard_map/ppermute | solution.py:23
  18.5 4.8 %collective-permute-start.4 = (bf16[128,128]{1,0:T(8,128)(2,1)S(1)}, bf16[128,128]{1,0:T(8,128)(2,1)S(1)}, u32[]{:S(2)}, u32[]{:S(2)}) collective-permute-start(bf16[128,128]{1,0:T(8,128)(2,1)S(1)} %get-tuple-element.24.after_ref.rest_0_), channel_id=1, source_target_pairs={{0,2},{1,3},{2,0},{3,1},{4,6},{5,7},{6,4},{7,5},{8,10},{9,11},{10,... | collective-permute-start | bytes 98312 | tf_op jit(solution)/shard_map/ppermute | solution.py:23
  21.0 2.8 %collective-permute-start.3 = (bf16[128,128]{1,0:T(8,128)(2,1)S(1)}, bf16[128,128]{1,0:T(8,128)(2,1)S(1)}, u32[]{:S(2)}, u32[]{:S(2)}) collective-permute-start(bf16[128,128]{1,0:T(8,128)(2,1)S(1)} %get-tuple-element.24.after_ref.rest_0_), channel_id=1, source_target_pairs={{0,1},{1,0},{2,3},{3,2},{4,5},{5,4},{6,7},{7,6},{8,9},{9,8},{10,11... | collective-permute-start | bytes 98312 | tf_op jit(solution)/shard_map/ppermute | solution.py:23
  21.0 4.2 %collective-permute-start.14 = (bf16[2,128,128]{2,1,0:T(8,128)(2,1)S(1)}, bf16[2,128,128]{2,1,0:T(8,128)(2,1)S(1)}, u32[]{:S(2)}, u32[]{:S(2)}) collective-permute-start(bf16[2,128,128]{2,1,0:T(8,128)(2,1)S(1)} %collective-permute-done.10.rest_9_), channel_id=1, source_target_pairs={{0,1},{1,0},{2,3},{3,2},{4,5},{5,4},{6,7},{7,6},{8,9},{9,8},{10,11... | collective-permute-start | bytes 196616 | tf_op jit(solution)/shard_map/ppermute | solution.py:23
  22.4 1.5 %collective-permute-start.9 = (bf16[128,128]{1,0:T(8,128)(2,1)S(1)}, bf16[128,128]{1,0:T(8,128)(2,1)S(1)}, u32[]{:S(2)}, u32[]{:S(2)}) collective-permute-start(bf16[128,128]{1,0:T(8,128)(2,1)S(1)} %collective-permute-done.8.rest_6_), channel_id=1, source_target_pairs={{0,1},{1,0},{2,3},{3,2},{4,5},{5,4},{6,7},{7,6},{8,9},{9,8},{10,11... | collective-permute-start | bytes 98312 | tf_op jit(solution)/shard_map/ppermute | solution.py:23
  23.3 1.9 %collective-permute-start.15 = (bf16[2,128,128]{2,1,0:T(8,128)(2,1)S(1)}, bf16[2,128,128]{2,1,0:T(8,128)(2,1)S(1)}, u32[]{:S(2)}, u32[]{:S(2)}) collective-permute-start(bf16[2,128,128]{2,1,0:T(8,128)(2,1)S(1)} %collective-permute-done.11.rest_10_), channel_id=1, source_target_pairs={{0,1},{1,0},{2,3},{3,2},{4,5},{5,4},{6,7},{7,6},{8,9},{9,8},{10,11... | collective-permute-start | bytes 196616 | tf_op jit(solution)/shard_map/ppermute | solution.py:23
  23.3 1.9 %collective-permute-start.16 = (bf16[2,128,128]{2,1,0:T(8,128)(2,1)S(1)}, bf16[2,128,128]{2,1,0:T(8,128)(2,1)S(1)}, u32[]{:S(2)}, u32[]{:S(2)}) collective-permute-start(bf16[2,128,128]{2,1,0:T(8,128)(2,1)S(1)} %collective-permute-done.12.rest_11_), channel_id=1, source_target_pairs={{0,1},{1,0},{2,3},{3,2},{4,5},{5,4},{6,7},{7,6},{8,9},{9,8},{10,11... | collective-permute-start | bytes 196616 | tf_op jit(solution)/shard_map/ppermute | solution.py:23
  23.8 1.2 %collective-permute-start.7 = (bf16[128,128]{1,0:T(8,128)(2,1)S(1)}, bf16[128,128]{1,0:T(8,128)(2,1)S(1)}, u32[]{:S(2)}, u32[]{:S(2)}) collective-permute-start(bf16[128,128]{1,0:T(8,128)(2,1)S(1)} %collective-permute-done.6.rest_4_), channel_id=1, source_target_pairs={{0,1},{1,0},{2,3},{3,2},{4,5},{5,4},{6,7},{7,6},{8,9},{9,8},{10,11... | collective-permute-start | bytes 98312 | tf_op jit(solution)/shard_map/ppermute | solution.py:23
  23.8 1.3 %collective-permute-start.5 = (bf16[128,128]{1,0:T(8,128)(2,1)S(1)}, bf16[128,128]{1,0:T(8,128)(2,1)S(1)}, u32[]{:S(2)}, u32[]{:S(2)}) collective-permute-start(bf16[128,128]{1,0:T(8,128)(2,1)S(1)} %collective-permute-done.4.rest_2_), channel_id=1, source_target_pairs={{0,1},{1,0},{2,3},{3,2},{4,5},{5,4},{6,7},{7,6},{8,9},{9,8},{10,11... | collective-permute-start | bytes 98312 | tf_op jit(solution)/shard_map/ppermute | solution.py:23
  30.9 4.5 %collective-permute-start.17 = (bf16[2,144,128]{2,1,0:T(8,128)(2,1)S(1)}, bf16[2,144,128]{2,1,0:T(8,128)(2,1)S(1)}, u32[]{:S(2)}, u32[]{:S(2)}) collective-permute-start(bf16[2,144,128]{2,1,0:T(8,128)(2,1)S(1)} %get-tuple-element.34), channel_id=1, source_target_pairs={{0,2},{1,3},{2,0},{3,1},{4,6},{5,7},{6,4},{7,5},{8,10},{9,11},{10,... | collective-permute-start | bytes 221192 | tf_op jit(solution)/shard_map/ppermute | solution.py:23
  32.3 8.6 %collective-permute-start.18 = (bf16[2,144,128]{2,1,0:T(8,128)(2,1)S(1)}, bf16[2,144,128]{2,1,0:T(8,128)(2,1)S(1)}, u32[]{:S(2)}, u32[]{:S(2)}) collective-permute-start(bf16[2,144,128]{2,1,0:T(8,128)(2,1)S(1)} %get-tuple-element.35), channel_id=1, source_target_pairs={{0,4},{1,5},{2,6},{3,7},{4,0},{5,1},{6,2},{7,3},{8,12},{9,13},{10,... | collective-permute-start | bytes 221192 | tf_op jit(solution)/shard_map/ppermute | solution.py:23
  33.4 7.6 %collective-permute-start.19 = (bf16[2,144,128]{2,1,0:T(8,128)(2,1)S(1)}, bf16[2,144,128]{2,1,0:T(8,128)(2,1)S(1)}, u32[]{:S(2)}, u32[]{:S(2)}) collective-permute-start(bf16[2,144,128]{2,1,0:T(8,128)(2,1)S(1)} %get-tuple-element.36), channel_id=1, source_target_pairs={{0,6},{1,7},{2,4},{3,5},{4,2},{5,3},{6,0},{7,1},{8,14},{9,15},{10,... | collective-permute-start | bytes 221192 | tf_op jit(solution)/shard_map/ppermute | solution.py:23
  35.2 8.0 %collective-permute-start.20 = (bf16[2,144,128]{2,1,0:T(8,128)(2,1)S(1)}, bf16[2,144,128]{2,1,0:T(8,128)(2,1)S(1)}, u32[]{:S(2)}, u32[]{:S(2)}) collective-permute-start(bf16[2,144,128]{2,1,0:T(8,128)(2,1)S(1)} %get-tuple-element.33.rest_0_), channel_id=1, source_target_pairs={{0,1},{1,0},{2,3},{3,2},{4,5},{5,4},{6,7},{7,6},{8,9},{9,8},{10,11... | collective-permute-start | bytes 221192 | tf_op jit(solution)/shard_map/ppermute | solution.py:23
  35.4 8.4 %collective-permute-start.21 = (bf16[2,144,128]{2,1,0:T(8,128)(2,1)S(1)}, bf16[2,144,128]{2,1,0:T(8,128)(2,1)S(1)}, u32[]{:S(2)}, u32[]{:S(2)}) collective-permute-start(bf16[2,144,128]{2,1,0:T(8,128)(2,1)S(1)} %collective-permute-done.17.rest_1_), channel_id=1, source_target_pairs={{0,1},{1,0},{2,3},{3,2},{4,5},{5,4},{6,7},{7,6},{8,9},{9,8},{10,11... | collective-permute-start | bytes 221192 | tf_op jit(solution)/shard_map/ppermute | solution.py:23
  41.0 4.0 %collective-permute-start.22 = (bf16[2,144,128]{2,1,0:T(8,128)(2,1)S(1)}, bf16[2,144,128]{2,1,0:T(8,128)(2,1)S(1)}, u32[]{:S(2)}, u32[]{:S(2)}) collective-permute-start(bf16[2,144,128]{2,1,0:T(8,128)(2,1)S(1)} %collective-permute-done.18.rest_2_), channel_id=1, source_target_pairs={{0,1},{1,0},{2,3},{3,2},{4,5},{5,4},{6,7},{7,6},{8,9},{9,8},{10,11... | collective-permute-start | bytes 221192 | tf_op jit(solution)/shard_map/ppermute | solution.py:23
  41.0 4.0 %collective-permute-start.23 = (bf16[2,144,128]{2,1,0:T(8,128)(2,1)S(1)}, bf16[2,144,128]{2,1,0:T(8,128)(2,1)S(1)}, u32[]{:S(2)}, u32[]{:S(2)}) collective-permute-start(bf16[2,144,128]{2,1,0:T(8,128)(2,1)S(1)} %collective-permute-done.19.rest_3_), channel_id=1, source_target_pairs={{0,1},{1,0},{2,3},{3,2},{4,5},{5,4},{6,7},{7,6},{8,9},{9,8},{10,11... | collective-permute-start | bytes 221192 | tf_op jit(solution)/shard_map/ppermute | solution.py:23
  41.5 5.9 %collective-permute-start.26 = (bf16[64,384]{1,0:T(8,128)(2,1)S(1)}, bf16[64,384]{1,0:T(8,128)(2,1)S(1)}, u32[]{:S(2)}, u32[]{:S(2)}) collective-permute-start(bf16[64,384]{1,0:T(8,128)(2,1)S(1)} %get-tuple-element.37.rest_0_), channel_id=1, source_target_pairs={{0,24},{8,16},{16,8},{24,0},{1,25},{9,17},{17,9},{25,1},{2,26},{10... | collective-permute-start | bytes 147464 | tf_op jit(solution)/shard_map/ppermute | solution.py:23
  43.3 5.3 %collective-permute-start.25 = (bf16[64,384]{1,0:T(8,128)(2,1)S(1)}, bf16[64,384]{1,0:T(8,128)(2,1)S(1)}, u32[]{:S(2)}, u32[]{:S(2)}) collective-permute-start(bf16[64,384]{1,0:T(8,128)(2,1)S(1)} %get-tuple-element.37.rest_0_), channel_id=1, source_target_pairs={{0,16},{8,24},{16,0},{24,8},{1,17},{9,25},{17,1},{25,9},{2,18},{10... | collective-permute-start | bytes 147464 | tf_op jit(solution)/shard_map/ppermute | solution.py:23
  43.8 4.8 %collective-permute-start.24 = (bf16[64,384]{1,0:T(8,128)(2,1)S(1)}, bf16[64,384]{1,0:T(8,128)(2,1)S(1)}, u32[]{:S(2)}, u32[]{:S(2)}) collective-permute-start(bf16[64,384]{1,0:T(8,128)(2,1)S(1)} %get-tuple-element.37.rest_0_), channel_id=1, source_target_pairs={{0,8},{8,0},{16,24},{24,16},{1,9},{9,1},{17,25},{25,17},{2,10},{10... | collective-permute-start | bytes 147464 | tf_op jit(solution)/shard_map/ppermute | solution.py:23
  45.0 5.5 %collective-permute-start.29 = (f32[8,128]{1,0:T(8,128)S(1)}, f32[8,128]{1,0:T(8,128)S(1)}, u32[]{:S(2)}, u32[]{:S(2)}) collective-permute-start(f32[8,128]{1,0:T(8,128)S(1)} %headsum.1.rest_0_), channel_id=1, source_target_pairs={{0,24},{8,16},{16,8},{24,0},{1,25},{9,17},{17,9},{25,1},{2,26},{10... | collective-permute-start | bytes 12296 | tf_op jit(solution)/shard_map/ppermute | solution.py:23
  46.9 3.7 %collective-permute-start.28 = (f32[8,128]{1,0:T(8,128)S(1)}, f32[8,128]{1,0:T(8,128)S(1)}, u32[]{:S(2)}, u32[]{:S(2)}) collective-permute-start(f32[8,128]{1,0:T(8,128)S(1)} %headsum.1.rest_0_), channel_id=1, source_target_pairs={{0,16},{8,24},{16,0},{24,8},{1,17},{9,25},{17,1},{25,9},{2,18},{10... | collective-permute-start | bytes 12296 | tf_op jit(solution)/shard_map/ppermute | solution.py:23
  47.4 3.6 %collective-permute-start.27 = (f32[8,128]{1,0:T(8,128)S(1)}, f32[8,128]{1,0:T(8,128)S(1)}, u32[]{:S(2)}, u32[]{:S(2)}) collective-permute-start(f32[8,128]{1,0:T(8,128)S(1)} %headsum.1.rest_0_), channel_id=1, source_target_pairs={{0,8},{8,0},{16,24},{24,16},{1,9},{9,1},{17,25},{25,17},{2,10},{10... | collective-permute-start | bytes 12296 | tf_op jit(solution)/shard_map/ppermute | solution.py:23
